TPU v7x, 128 devices: a whole 4x4x4 slice. The times are simulated.
128 devices in a mesh: kv: 2 (over y_lo), ctx: 64 (over z, x, y_hi, core).
Axes of the slice: x: 4, y: 4 (y_hi: 2, y_lo: 2; y = y_hi * 2 + y_lo), z: 4, core: 2. Of those that a mesh axis runs over, the one named last changes fastest.
Arguments:
- residual: bfloat16 [64, 8192], P(None, 'ctx'), may hold values from -8 to 8
- queries: bfloat16 [64, 8192], P(None, 'kv'), may hold values from -16 to 16
- draft_token_keys: bfloat16 [64, 1024], P(None, 'kv'), may hold values from -32 to 32
- draft_token_values: bfloat16 [64, 1024], P(None, 'kv'), may hold values from -8 to 8
- cache_keys: bfloat16 [2, 32768, 1024], P(None, 'ctx', 'kv'), may hold values from -32 to 32
- cached_value_rows: bfloat16 [2, 32768, 1024], P(None, 'ctx', 'kv'), may hold values from -8 to 8
- tenant_ids: int32 [64], replicated, may hold values from 0 to 1, as said below
- tree_mask: int32 [64, 64], replicated, may hold values from 0 to 1, as said below
- cache_lengths: int32 [2], replicated, may hold values from 16385 to 32768
- out_weight: bfloat16 [8192, 8192], P('kv', 'ctx'), may hold values from -0.0625 to 0.0625
- out_signs: bfloat16 [2, 8192, 8192], P(None, 'kv', 'ctx'), may hold values from -1 to 1, as said below
- norm_gain: float32 [8192], P('ctx'), may hold values from 0.1 to 1.9
- gate_weight: bfloat16 [8192, 16384], P(None, ('kv', 'ctx')), may hold values from -0.0625 to 0.0625
- up_weight: bfloat16 [8192, 16384], P(None, ('kv', 'ctx')), may hold values from -0.0625 to 0.0625
- down_weight: bfloat16 [16384, 8192], P(('kv', 'ctx')), may hold values from -0.1875 to 0.1875
- gate_signs: bfloat16 [2, 8192, 16384], P(None, None, ('kv', 'ctx')), may hold values from -1 to 1, as said below
- up_signs: bfloat16 [2, 8192, 16384], P(None, None, ('kv', 'ctx')), may hold values from -1 to 1, as said below
- down_signs: bfloat16 [2, 16384, 8192], P(None, ('kv', 'ctx')), may hold values from -1 to 1, as said below
- delta_scale: float32 [2, 4], replicated, may hold values from 0.3 to 0.9
Outputs:
- mixed: bfloat16 [64, 8192], P(None, 'ctx')
Inputs may be any that keep to these rules, and one draw needn't show every extreme that they name: `tenant_ids`: exactly 32 tokens belong to each tenant. `tree_mask`: entry (i, j) is 1 exactly when token j is token i or an ancestor of token i in the draft tree of their common tenant; each tenant's 32 tokens form one tree. `out_signs`: every entry is 1 or -1. `gate_signs`: every entry is 1 or -1. `up_signs`: every entry is 1 or -1. `down_signs`: every entry is 1 or -1.
All inputs are finite; a program needn't handle non-finite values.
Results may differ from a plain program's by a relative error of at most 0.013.
Values may be sent and summed in bfloat16 or wider, within the bound.
A program may use at most 128 MiB of HBM per device.

v0:
```python
import jax
import jax.numpy as jnp
from jax import lax
from jax.sharding import PartitionSpec as P

D = 8192
QUERY_HEADS = 64
HEAD_SIZE = 128
FF = 16384


NEG = -1e30
EPS = 1e-05


def sent_together(arrays, axis, split_dim, concat_dim, along):
    columns = [a.reshape(*a.shape[:along], -1) for a in arrays]
    both = jnp.concatenate(columns, axis=along)
    filled, at, done = (
        lax.all_to_all(both, axis, split_axis=split_dim, concat_axis=concat_dim, tiled=True),
        0,
        [],
    )
    for a, column in zip(arrays, columns):
        share = filled[..., at : at + column.shape[along]]
        done.append(share.reshape(*share.shape[:along], *a.shape[along:]))
        at += column.shape[along]
    return tuple(done)


def sent_to_all(shard, axis):
    copies = jnp.broadcast_to(shard, (lax.axis_size(axis), *shard.shape))
    return lax.all_to_all(copies, axis, split_axis=0, concat_axis=0, tiled=True)


def laid_out(tiles, dim):
    tiles = jnp.moveaxis(tiles, 0, dim)
    shape = tiles.shape
    return tiles.reshape(*shape[:dim], shape[dim] * shape[dim + 1], *shape[dim + 2 :])


def collect(shard, axis, dim):
    tiles = sent_to_all(shard, axis)
    return laid_out(tiles, dim)


def of_everyone(shard, axis):
    return sent_to_all(shard, axis).astype(jnp.float32).sum(axis=0)


def of_everyone_2(shard, axis):
    everything = sent_to_all(shard, axis)
    return jnp.sum(everything, axis=0)


def cut_along(shard, dim, peers):
    before, after = (shard.shape[:dim], shard.shape[dim + 1 :])
    return jnp.moveaxis(shard.reshape(*before, peers, -1, *after), dim, 0)


def sum_at_owner(shard, axis, dim):
    tiles = cut_along(shard, dim, lax.axis_size(axis))
    arrived = lax.all_to_all(tiles, axis, split_axis=0, concat_axis=0, tiled=True)
    return arrived.sum(axis=0)


def combine(first, second):
    first_top, first_total, first_out = first
    second_top, second_total, second_out = second
    peak = jnp.maximum(first_top, second_top)
    first_scale = jnp.exp(first_top - peak)
    second_scale = jnp.exp(second_top - peak)
    total = first_total * first_scale + second_total * second_scale
    merged = first_out * first_scale[..., None] + second_out * second_scale[..., None]
    return (peak, total, merged)


def draft_rows(query_rows, group_rows, visible_rows, key_rows, value_rows, factor):
    groups = key_rows.shape[1]
    choose = (group_rows[:, None] == jnp.arange(groups, dtype=jnp.int32)[None, :]).astype(
        jnp.float32
    )
    every_group = (
        jnp.einsum("rd,kgd->rgk", query_rows, key_rows, preferred_element_type=jnp.float32) * factor
    )
    scores = jnp.einsum("rgk,rg->rk", every_group, choose, precision=lax.Precision.HIGHEST)
    masked = jnp.where(visible_rows, scores, NEG)
    peak = jnp.max(masked, axis=-1)
    weights = jnp.where(visible_rows, jnp.exp(masked - peak[:, None]), 0.0)
    total = jnp.sum(weights, axis=-1)
    every_value = jnp.einsum(
        "rk,kgd->rgd", weights.astype(jnp.bfloat16), value_rows, preferred_element_type=jnp.float32
    )
    result = jnp.einsum("rgd,rg->rd", every_value, choose, precision=lax.Precision.HIGHEST)
    return (peak, total, result)


def shards(
    residual,
    queries,
    draft_token_keys,
    draft_token_values,
    cache_keys,
    cached_value_rows,
    tenant_ids,
    tree_mask,
    cache_lengths,
    out_weight,
    out_signs,
    norm_gain,
    gate_weight,
    up_weight,
    down_weight,
    gate_signs,
    up_signs,
    down_signs,
    delta_scale,
):
    tenants = cache_keys.shape[0]
    tokens = tenant_ids.shape[0]
    draft = tokens // tenants
    heads_here = queries.shape[1] // HEAD_SIZE
    groups_here = draft_token_keys.shape[1] // HEAD_SIZE
    group_width = heads_here // groups_here
    ctx_rows = cache_keys.shape[1]
    factor = HEAD_SIZE ** (-0.5)
    sort_order = jnp.argsort(tenant_ids, stable=True)
    inverse = jnp.argsort(sort_order)
    sorted_queries = queries[sort_order]
    query_blocks = sorted_queries.reshape(tenants, draft, groups_here, group_width, HEAD_SIZE)
    draft_key_lines = draft_token_keys[sort_order].reshape(tokens, groups_here, HEAD_SIZE)
    draft_value_lines = draft_token_values[sort_order].reshape(tokens, groups_here, HEAD_SIZE)
    visible = tree_mask[sort_order][:, sort_order] > 0
    first_slot = lax.axis_index("ctx") * ctx_rows
    slot_ids = first_slot + jnp.arange(ctx_rows, dtype=jnp.int32)
    live = (slot_ids[None, :] < cache_lengths[:, None])[:, None, None, None, :]
    cache_key_blocks = cache_keys.reshape(tenants, ctx_rows, groups_here, HEAD_SIZE)
    cache_value_blocks = cached_value_rows.reshape(tenants, ctx_rows, groups_here, HEAD_SIZE)
    scores = (
        jnp.einsum(
            "tqgwd,tjgd->tqgwj", query_blocks, cache_key_blocks, preferred_element_type=jnp.float32
        )
        * factor
    )
    masked = jnp.where(live, scores, NEG)
    peak = jnp.max(masked, axis=-1)
    weights = jnp.where(live, jnp.exp(masked - peak[..., None]), 0.0)
    total = jnp.sum(weights, axis=-1)
    weighted = jnp.einsum(
        "tqgwj,tjgd->tqgwd",
        weights.astype(jnp.bfloat16),
        cache_value_blocks,
        preferred_element_type=jnp.float32,
    )
    part_top = peak.reshape(tokens, heads_here)
    part_total = total.reshape(tokens, heads_here)
    part_out = weighted.reshape(tokens, heads_here, HEAD_SIZE)
    n_ctx = lax.axis_size("ctx")
    all_rows = tokens * heads_here
    share = all_rows // n_ctx
    got_top, got_total, got_out = (
        lax.all_to_all(
            part_top.reshape(1, all_rows), "ctx", split_axis=1, concat_axis=0, tiled=True
        ),
        *sent_together(
            (part_total.reshape(1, all_rows), part_out.reshape(1, all_rows, HEAD_SIZE)),
            "ctx",
            1,
            0,
            2,
        ),
    )
    summit = jnp.max(got_top, axis=0)
    rescale = jnp.exp(got_top - summit)
    merged = (
        summit,
        jnp.sum(got_total * rescale, axis=0),
        jnp.sum(got_out * rescale[..., None], axis=0),
    )
    first_row = lax.axis_index("ctx") * share
    row_ids = first_row + jnp.arange(share, dtype=jnp.int32)
    token_rows = row_ids // heads_here
    group_rows = row_ids % heads_here // group_width
    query_rows = lax.dynamic_slice_in_dim(
        sorted_queries.reshape(all_rows, HEAD_SIZE), first_row, share, 0
    )
    own = draft_rows(
        query_rows, group_rows, visible[token_rows], draft_key_lines, draft_value_lines, factor
    )
    final_top, final_total, final_out = combine(merged, own)
    finished = (final_out / final_total[:, None]).astype(jnp.bfloat16)
    attention = collect(finished, "ctx", 0).reshape(tokens, heads_here * HEAD_SIZE)
    attention_split = attention.reshape(tenants, draft, -1)
    projected = jnp.dot(attention, out_weight, preferred_element_type=jnp.float32)
    out_delta = jnp.einsum(
        "tqh,thf->tqf", attention_split, out_signs, preferred_element_type=jnp.float32
    )
    projected = projected + (
        out_delta * (delta_scale[:, 0] * (QUERY_HEADS * HEAD_SIZE) ** (-0.5))[:, None, None]
    ).reshape(tokens, -1)
    summed_heads = of_everyone(projected.astype(jnp.bfloat16), "kv").astype(jnp.float32)
    hidden = residual[sort_order].astype(jnp.float32) + summed_heads
    squares = of_everyone_2(jnp.sum(hidden * hidden, axis=1), "ctx")
    normed = (hidden * lax.rsqrt(squares / D + EPS)[:, None] * norm_gain).astype(jnp.bfloat16)
    hidden_units = gate_weight.shape[1]
    piece = lax.all_gather(normed, "ctx", axis=1, tiled=True)
    size = piece.shape[1]
    split_piece = piece.reshape(tenants, draft, size)
    gate_base = jnp.dot(piece, gate_weight, preferred_element_type=jnp.float32)
    up_base = jnp.dot(piece, up_weight, preferred_element_type=jnp.float32)
    gate_delta = jnp.einsum(
        "tqf,tfh->tqh", split_piece, gate_signs, preferred_element_type=jnp.float32
    )
    up_delta = jnp.einsum("tqf,tfh->tqh", split_piece, up_signs, preferred_element_type=jnp.float32)
    gate = gate_base + (gate_delta * (delta_scale[:, 1] * D ** (-0.5))[:, None, None]).reshape(
        tokens, hidden_units
    )
    up_part = up_base + (up_delta * (delta_scale[:, 2] * D ** (-0.5))[:, None, None]).reshape(
        tokens, hidden_units
    )
    active = (jax.nn.silu(gate) * up_part).astype(jnp.bfloat16)
    active_split = active.reshape(tenants, draft, hidden_units)
    down_factor = delta_scale[:, 3] * FF ** (-0.5)
    features_here = residual.shape[1]
    base_part = lax.dot_general(
        down_weight, active, (((0,), (1,)), ((), ())), preferred_element_type=jnp.float32
    )
    delta_part = jnp.einsum(
        "thf,tqh->ftq", down_signs, active_split, preferred_element_type=jnp.float32
    )
    delta_part = delta_part * down_factor[None, :, None]
    lowered = sum_at_owner(
        base_part + delta_part.reshape(features_here * lax.axis_size("ctx"), tokens), "ctx", 0
    )
    lowered = of_everyone(lowered.astype(jnp.bfloat16), "kv").astype(jnp.float32)
    return (hidden + lowered.T).astype(jnp.bfloat16)[inverse]


def solution(mesh):
    return jax.shard_map(
        shards,
        mesh=mesh,
        in_specs=(
            P(None, "ctx"),
            P(None, "kv"),
            P(None, "kv"),
            P(None, "kv"),
            P(None, "ctx", "kv"),
            P(None, "ctx", "kv"),
            P(),
            P(),
            P(),
            P("kv", "ctx"),
            P(None, "kv", "ctx"),
            P("ctx"),
            P(None, ("kv", "ctx")),
            P(None, ("kv", "ctx")),
            P(("kv", "ctx"), None),
            P(None, None, ("kv", "ctx")),
            P(None, None, ("kv", "ctx")),
            P(None, ("kv", "ctx"), None),
            P(),
        ),
        out_specs=P(None, "ctx"),
        check_vma=False,
    )
```

profile of v0, /device:TPU:0, one launch (start us, length us, event | category | flops | bytes accessed | tf_op | source)
XLA Modules:
  0.0 268.2 jit_solution(5693490985125798498)
XLA Ops:
  6.5 2.8 %sort.34 = (s32[64]{0:T(128)}, s32[64]{0:T(128)S(1)}) sort(s32[64]{0:T(128)} %param.25, s32[64]{0:T(128)S(1)} %iota.25), dimensions={0}, to_apply=%region_0.0 | sort | flops 384 | bytes 1024 | tf_op jit(solution)/shard_map/jit(argsort)/sort | solution.py:127
  9.4 2.2 reshape.251
  12.6 4.0 %bitcast_reduce_fusion = (f32[2,32,4,8]{3,1,2,0:T(8,128)S(1)}, f32[2,4,32,8,512]{4,3,2,1,0:T(8,128)}) fusion(pred[2,512]{1,0:T(4,128)(4,1)S(1)} %broadcast_compare_fusion, bf16[2,512,4,128,1]{3,2,1,0,4:T(4,128)(2,1)} %bitcast.117, bf16[2,32,4,8,128]{4,3,2,1,0:T(8,128)(2,1)S(1)} %bitcast.119), kind=kOutput, calls=%fused_computation.12 | convolution fusion | flops 271579136 | bytes 5776384 | tf_op jit(solution)/shard_map/tqgwd,tjgd->tqgwj/dot_general | solution.py:140
  17.5 11.5 %all-to-all-start.1 = ((f32[1,64,32]{2,0,1:T(1,128)}), f32[1,64,32]{2,0,1:T(1,128)S(1)}, u32[]{:S(2)}, u32[]{:S(2)}) async-start(f32[1,64,32]{2,0,1:T(1,128)} %copy.96), calls=%async_computation.1 | async-start | bytes 65536 | tf_op jit(solution)/shard_map/all_to_all | solution.py:162
  33.5 3.5 %fusion.4 = f32[2,32,4,8]{3,1,2,0:T(8,128)S(1)} fusion(f32[2,4,32,8,512]{4,3,2,1,0:T(8,128)} %get-tuple-element.19, f32[2,32,4,8]{3,1,2,0:T(8,128)S(1)} %get-tuple-element.18, pred[2,512]{1,0:T(4,128)(4,1)S(1)} %broadcast_compare_fusion), kind=kLoop, calls=%fused_computation.17 | loop fusion | flops 5240832 | bytes 4211712 | tf_op jit(solution)/shard_map/reduce_sum | solution.py:148
  39.9 3.2 %pad_maximum_fusion = f32[1,2048,129]{2,1,0:T(8,128)} fusion(f32[1,2048,128]{2,1,0:T(8,128)S(1)} %bitcast.118, f32[1,2048,1]{2,1,0:T(8,128)} %reshape_reshape_reshape.8), kind=kLoop, calls=%fused_computation.19 | loop fusion | flops 264192 | bytes 2113536 | tf_op jit(solution)/shard_map/concatenate | solution.py:18
  44.8 4.8 %copy.94 = f32[1,2048,129]{2,0,1:T(1,128)} copy(f32[1,2048,129]{2,1,0:T(8,128)} %pad_maximum_fusion) | data formatting | bytes 2113536 | tf_op jit(solution)/shard_map/concatenate | solution.py:18
  50.2 10.6 %all-to-all-start = ((f32[1,2048,129]{2,0,1:T(1,128)}), f32[1,2048,129]{2,0,1:T(1,128)}, u32[]{:S(2)}, u32[]{:S(2)}) async-start(f32[1,2048,129]{2,0,1:T(1,128)} %copy.94), calls=%async_computation | async-start | bytes 4194304 | tf_op jit(solution)/shard_map/all_to_all | solution.py:20
  62.1 28.9 %all-to-all-done = f32[1,2048,129]{2,0,1:T(1,128)} async-done(((f32[1,2048,129]{2,0,1:T(1,128)}), f32[1,2048,129]{2,0,1:T(1,128)}, u32[]{:S(2)}, u32[]{:S(2)}) %all-to-all-start) | async-done | bytes 1056800 | tf_op jit(solution)/shard_map/all_to_all | solution.py:20
  95.0 2.2 fusion.17
  98.2 5.5 %all-to-all-start.2 = ((bf16[64,32,128]{2,1,0:T(8,128)(2,1)}), bf16[64,32,128]{2,1,0:T(8,128)(2,1)S(1)}, u32[]{:S(2)}, u32[]{:S(2)}) async-start(bf16[64,32,128]{2,1,0:T(8,128)(2,1)} %broadcast_in_dim.76), calls=%async_computation.2 | async-start | bytes 1048576 | tf_op jit(solution)/shard_map/all_to_all | solution.py:33
  104.0 13.7 %all-to-all-done.2 = bf16[64,32,128]{2,1,0:T(8,128)(2,1)S(1)} async-done(((bf16[64,32,128]{2,1,0:T(8,128)(2,1)}), bf16[64,32,128]{2,1,0:T(8,128)(2,1)S(1)}, u32[]{:S(2)}, u32[]{:S(2)}) %all-to-all-start.2) | async-done | bytes 524320 | tf_op jit(solution)/shard_map/all_to_all | solution.py:33
  117.9 2.0 convolution_multiply_fusion.4
  122.2 3.3 %all-to-all-start.3 = ((bf16[2,64,128]{2,1,0:T(8,128)(2,1)}), bf16[2,64,128]{2,1,0:T(8,128)(2,1)S(1)}, u32[]{:S(2)}, u32[]{:S(2)}) async-start(bf16[2,64,128]{2,1,0:T(8,128)(2,1)} %broadcast_in_dim.77), calls=%async_computation.3 | async-start | bytes 65536 | tf_op jit(solution)/shard_map/all_to_all | solution.py:33
  126.1 3.2 %all-to-all-done.3 = bf16[2,64,128]{2,1,0:T(8,128)(2,1)S(1)} async-done(((bf16[2,64,128]{2,1,0:T(8,128)(2,1)}), bf16[2,64,128]{2,1,0:T(8,128)(2,1)S(1)}, u32[]{:S(2)}, u32[]{:S(2)}) %all-to-all-start.3) | async-done | bytes 32800 | tf_op jit(solution)/shard_map/all_to_all | solution.py:33
  129.5 13.8 %all_to_all.54 = f32[64,1,64]{2,1,0:T(1,128)S(1)} all-to-all(f32[64,1,64]{2,1,0:T(1,128)S(1)} %broadcast_in_dim.78), channel_id=1, replica_groups=mesh['kv'=2,'ctx'=64] {'ctx'}, dimensions={0} | all-to-all | bytes 32768 | tf_op jit(solution)/shard_map/all_to_all | solution.py:33
  144.1 57.7 %all-gather.2.cloned.1.call-done = bf16[64,8192]{1,0:T(8,128)(2,1)} async-done(((bf16[64,128]{1,0:T(8,128)(2,1)}), bf16[64,8192]{1,0:T(8,128)(2,1)}) %all-gather.2.cloned.1.call-update) | async-done | bytes 1048592 | tf_op jit(solution)/shard_map/all_gather | solution.py:206
  201.8 3.4 %convolution_multiply_fusion.2 = f32[2,32,128]{2,1,0:T(8,128)S(1)} fusion(bf16[2,32,8192]{2,1,0:T(8,128)(2,1)} %bitcast.109, bf16[2,8192,128]{2,1,0:T(8,128)(2,1)} %param.35, f32[2]{0:T(128)S(1)} %get-tuple-element.12), kind=kOutput, calls=%fused_computation.27 | convolution fusion | flops 134225920 | bytes 5275656 | tf_op jit(solution)/shard_map/tqf,tfh->tqh/dot_general | solution.py:214
  211.8 8.6 %all-to-all-start.5 = ((f32[64,128,64]{1,2,0:T(8,128)}), f32[64,128,64]{1,2,0:T(8,128)}, u32[]{:S(2)}, u32[]{:S(2)}) async-start(f32[64,128,64]{1,2,0:T(8,128)} %bitcast.112), calls=%async_computation.5 | async-start | bytes 4194304 | tf_op jit(solution)/shard_map/all_to_all | solution.py:63
  220.4 2.0 sort.35
  222.4 28.1 %all-to-all-done.5 = f32[64,128,64]{1,2,0:T(8,128)} async-done(((f32[64,128,64]{1,2,0:T(8,128)}), f32[64,128,64]{1,2,0:T(8,128)}, u32[]{:S(2)}, u32[]{:S(2)}) %all-to-all-start.5) | async-done | bytes 2097184 | tf_op jit(solution)/shard_map/all_to_all | solution.py:63
  250.5 1.7 reduce_sum.88
  252.9 3.3 %all-to-all-start.6 = ((bf16[2,128,64]{1,2,0:T(8,128)(2,1)}), bf16[2,128,64]{1,2,0:T(8,128)(2,1)S(1)}, u32[]{:S(2)}, u32[]{:S(2)}) async-start(bf16[2,128,64]{1,2,0:T(8,128)(2,1)} %broadcast_in_dim.79), calls=%async_computation.6 | async-start | bytes 65536 | tf_op jit(solution)/shard_map/all_to_all | solution.py:33
  256.2 3.9 %all-to-all-done.6 = bf16[2,128,64]{1,2,0:T(8,128)(2,1)S(1)} async-done(((bf16[2,128,64]{1,2,0:T(8,128)(2,1)}), bf16[2,128,64]{1,2,0:T(8,128)(2,1)S(1)}, u32[]{:S(2)}, u32[]{:S(2)}) %all-to-all-start.6) | async-done | bytes 32800 | tf_op jit(solution)/shard_map/all_to_all | solution.py:33
  (103 shorter events, 30.3 us)
Async XLA Ops:
  6.5 203.2 %copy-start = (bf16[128,8192]{1,0:T(8,128)(2,1)S(1)}, bf16[128,8192]{1,0:T(8,128)(2,1)}, u32[]{:S(2)}) copy-start(bf16[128,8192]{1,0:T(8,128)(2,1)} %param.33) | copy-start | bytes 6291460
  6.5 5.0 %copy-start.2 = (bf16[64,4096]{1,0:T(8,128)(2,1)S(1)}, bf16[64,4096]{1,0:T(8,128)(2,1)}, u32[]{:S(2)}) copy-start(bf16[64,4096]{1,0:T(8,128)(2,1)} %param.20) | copy-start | bytes 1572868
  6.5 6.0 %copy-start.15 = (s32[2]{0:T(128)S(1)}, s32[2]{0:T(128)}, u32[]{:S(2)}) copy-start(s32[2]{0:T(128)} %param.27) | copy-start | bytes 28
  12.4 17.6 %copy-start.9 = (s32[64,64]{1,0:T(8,128)S(1)}, s32[64,64]{1,0:T(8,128)}, u32[]{:S(2)}) copy-start(s32[64,64]{1,0:T(8,128)} %param.26) | copy-start | bytes 49156
  12.6 18.8 %copy-start.7 = (bf16[64,512]{1,0:T(8,128)(2,1)S(1)}, bf16[64,512]{1,0:T(8,128)(2,1)}, u32[]{:S(2)}) copy-start(bf16[64,512]{1,0:T(8,128)(2,1)} %param.21) | copy-start | bytes 196612
  17.5 32.7 %all-to-all-start.1 = ((f32[1,64,32]{2,0,1:T(1,128)}), f32[1,64,32]{2,0,1:T(1,128)S(1)}, u32[]{:S(2)}, u32[]{:S(2)}) async-start(f32[1,64,32]{2,0,1:T(1,128)} %copy.96), calls=%async_computation.1 | async-start | bytes 65536 | tf_op jit(solution)/shard_map/all_to_all | solution.py:162
  33.5 3.5 %copy-start.3 = (f32[2,4,32,8,512]{4,3,2,1,0:T(8,128)S(1)}, f32[2,4,32,8,512]{4,3,2,1,0:T(8,128)}, u32[]{:S(2)}) copy-start(f32[2,4,32,8,512]{4,3,2,1,0:T(8,128)} %get-tuple-element.19) | copy-start | bytes 12582916
  38.3 5.7 %copy-start.8 = (bf16[64,512]{1,0:T(8,128)(2,1)S(1)}, bf16[64,512]{1,0:T(8,128)(2,1)}, u32[]{:S(2)}) copy-start(bf16[64,512]{1,0:T(8,128)(2,1)} %param.22) | copy-start | bytes 196612
  50.2 40.8 %all-to-all-start = ((f32[1,2048,129]{2,0,1:T(1,128)}), f32[1,2048,129]{2,0,1:T(1,128)}, u32[]{:S(2)}, u32[]{:S(2)}) async-start(f32[1,2048,129]{2,0,1:T(1,128)} %copy.94), calls=%async_computation | async-start | bytes 4194304 | tf_op jit(solution)/shard_map/all_to_all | solution.py:20
  62.1 41.7 %copy-start.13 = (f32[2,4]{1,0:T(2,128)S(1)}, f32[2,4]{1,0:T(2,128)}, u32[]{:S(2)}) copy-start(f32[2,4]{1,0:T(2,128)} %param.37) | copy-start | bytes 100
  92.7 1.4 copy-start.4
  94.7 30.7 %copy-start.12 = (bf16[64,128]{1,0:T(8,128)(2,1)S(1)}, bf16[64,128]{1,0:T(8,128)(2,1)}, u32[]{:S(2)}) copy-start(bf16[64,128]{1,0:T(8,128)(2,1)} %param.19) | copy-start | bytes 49156
  95.0 48.4 %copy-start.14 = (f32[128]{0:T(128)S(1)}, f32[128]{0:T(128)}, u32[]{:S(2)}) copy-start(f32[128]{0:T(128)} %param.30) | copy-start | bytes 1540
  98.2 19.5 %all-to-all-start.2 = ((bf16[64,32,128]{2,1,0:T(8,128)(2,1)}), bf16[64,32,128]{2,1,0:T(8,128)(2,1)S(1)}, u32[]{:S(2)}, u32[]{:S(2)}) async-start(bf16[64,32,128]{2,1,0:T(8,128)(2,1)} %broadcast_in_dim.76), calls=%async_computation.2 | async-start | bytes 1048576 | tf_op jit(solution)/shard_map/all_to_all | solution.py:33
  122.2 7.2 %all-to-all-start.3 = ((bf16[2,64,128]{2,1,0:T(8,128)(2,1)}), bf16[2,64,128]{2,1,0:T(8,128)(2,1)S(1)}, u32[]{:S(2)}, u32[]{:S(2)}) async-start(bf16[2,64,128]{2,1,0:T(8,128)(2,1)} %broadcast_in_dim.77), calls=%async_computation.3 | async-start | bytes 65536 | tf_op jit(solution)/shard_map/all_to_all | solution.py:33
  125.4 76.3 %all-gather.2.cloned.1.call-start = ((), (), s32[]{:S(2)}) async-start(), calls=%async_computation.7 | async-start | bytes 1064960 | tf_op jit(solution)/shard_map/all_gather | solution.py:206
  201.8 3.4 %copy-start.1 = (bf16[64,8192]{1,0:T(8,128)(2,1)S(1)}, bf16[64,8192]{1,0:T(8,128)(2,1)}, u32[]{:S(2)}) copy-start(bf16[64,8192]{1,0:T(8,128)(2,1)} %all-gather.2.cloned.1.call-done) | copy-start | bytes 3145732
  201.8 4.1 %copy-start.5 = (bf16[2,8192,128]{2,1,0:T(8,128)(2,1)S(1)}, bf16[2,8192,128]{2,1,0:T(8,128)(2,1)}, u32[]{:S(2)}) copy-start(bf16[2,8192,128]{2,1,0:T(8,128)(2,1)} %param.34) | copy-start | bytes 12582916
  205.2 1.8 copy-start.10
  205.8 1.7 copy-start.11
  206.6 2.4 copy-start.6
  211.8 38.7 %all-to-all-start.5 = ((f32[64,128,64]{1,2,0:T(8,128)}), f32[64,128,64]{1,2,0:T(8,128)}, u32[]{:S(2)}, u32[]{:S(2)}) async-start(f32[64,128,64]{1,2,0:T(8,128)} %bitcast.112), calls=%async_computation.5 | async-start | bytes 4194304 | tf_op jit(solution)/shard_map/all_to_all | solution.py:63
  252.9 7.2 %all-to-all-start.6 = ((bf16[2,128,64]{1,2,0:T(8,128)(2,1)}), bf16[2,128,64]{1,2,0:T(8,128)(2,1)S(1)}, u32[]{:S(2)}, u32[]{:S(2)}) async-start(bf16[2,128,64]{1,2,0:T(8,128)(2,1)} %broadcast_in_dim.79), calls=%async_computation.6 | async-start | bytes 65536 | tf_op jit(solution)/shard_map/all_to_all | solution.py:33
Sparse Core Ops, SparseCore 0:
  144.2 57.4 all-gather.1
where the time goes:
time: 269 us; the launch traced here: 268 us
  waiting for transfers between devices  135 us (50%)
  starting transfers between devices  42.8 us (16%)
  local copies, waits for them, and re-layouts  27.9 us (10%)
  other arithmetic  17.5 us (7%)
  matrix products  16.8 us (6%)
  blocking collectives  13.8 us (5%)
  between operations  13.8 us (5%)
    all_gather x1, waiting for transfers between devices, shards(): piece = lax.all_gather(normed, 'ctx', axis=1, tiled=True)  57.7 us
    all_to_all x1, waiting for transfers between devices, sent_together(): lax.all_to_all(both, axis, split_axis=split_dim, concat_axis=concat_dim,...  28.9 us
    all_to_all x1, waiting for transfers between devices, sum_at_owner(): lax.all_to_all(tiles, axis, split_axis=0, concat_axis=0, tiled=True)  28.1 us
    all_to_all x3, waiting for transfers between devices, sent_to_all(): return lax.all_to_all(copies, axis, split_axis=0, concat_axis=0, tiled=True)  20.9 us
    all_to_all x1, blocking collectives, sent_to_all(): return lax.all_to_all(copies, axis, split_axis=0, concat_axis=0, tiled=True)  13.8 us
    all_to_all x3, starting transfers between devices, sent_to_all(): return lax.all_to_all(copies, axis, split_axis=0, concat_axis=0, tiled=True)  12.1 us
    all_to_all x1, starting transfers between devices, shards(): lax.all_to_all(part_top.reshape(1, all_rows), 'ctx', split_axis=1, concat...  11.5 us
    all_to_all x1, starting transfers between devices, sent_together(): lax.all_to_all(both, axis, split_axis=split_dim, concat_axis=concat_dim,...  10.6 us
  transfers between devices with their start and end apart: 7, of which 6 were waited for; matrix products, arithmetic and copies ran while one was open for 9% of the time, Pallas kernels for 0%

commit v1 on v0

v1 whole, which is shorter than its diff:
```python
import functools

import jax
import jax.numpy as jnp
from jax import lax
from jax.experimental import pallas as pl
from jax.experimental.pallas import tpu as pltpu
from jax.sharding import PartitionSpec as P

D = 8192
FF = 16384
HEAD = 128
SLOTS = 512
NEG = -1e30
EPS = 1e-05
MESH = pl.DeviceIdType.MESH
f32, bf16, i32 = jnp.float32, jnp.bfloat16, jnp.int32
ORDER = (2, 1, 3)
NEAR = (1, 3, 2)


def dot(a, b, dims=((1,), (0,))):
    return lax.dot_general(a, b, (dims, ((), ())), preferred_element_type=f32)


def mult(v, n):
    return pl.multiple_of(v, n)


def lanes():
    return lax.broadcasted_iota(i32, (32, 128), 1)


def split(st):
    hi = st.astype(bf16).astype(f32)
    mid = (st - hi).astype(bf16).astype(f32)
    lo = st - hi - mid
    lane = lanes()
    return jnp.where(
        lane < 32, hi, jnp.where(lane < 64, mid, jnp.where(lane < 96, lo, 0.0))
    ).astype(bf16)


def join(block):
    v = block.astype(f32)
    v = v + pltpu.roll(v, 32, 1)
    return v + pltpu.roll(v, 64, 1)


def blend(stats):
    top = functools.reduce(jnp.maximum, stats)
    parts = [jnp.exp(s - top) for s in stats]
    total = functools.reduce(jnp.add, parts)
    inverse = 1.0 / total
    return [w * inverse for w in parts], top + jnp.log(total)


def mixed_of(factors, blocks, k):
    terms = [f[:, k : k + 1] * b for f, b in zip(factors, blocks)]
    return functools.reduce(jnp.add, terms)


def layer(
    ids_h, mask_h, lens, dsc, res_h, q_h, dk_h, dv_h, ck_h, cv_h, wo_h, so_h, gain_h,
    wg_h, wu_h, wd_h, sg_h, su_h, sd_h,
    out_ref,
    ids, mask, qraw, qs, kc, vc, dk, dv, vis, pm, pt, wo, so, wg, wu, wd, sg, su, sd,
    rres, gains, acs, acr, a1s, a1r, a2s, a2r, a3s, a3r, ab, yb, hid, gb, ss,
    ecs, ecr, e1o, e1s, e1r, e2s, e2r, e3s, e3r,
    ls, c_s, c_r, a1_s, a1_r, a2_s, a2_r, a3_s, a3_r, r_s, r_r,
    bq_s, bq_r, bp_s, bp_r, bc_s, bc_r, y_s, y_r,
    dq_s, dq_r, dp_s, dp_r, dc_s, dc_r, n_s, n_r,
    e0_s, e0_r, e1_s, e1_r, e2_s, e2_r, e3_s, e3_r,
):
    kv, ctx = lax.axis_index("kv"), lax.axis_index("ctx")
    c = ctx % 2
    yh = (ctx // 2) % 2
    x = (ctx // 4) % 4
    z = ctx // 16
    p = z + c * (x - z)
    q = x + c * (z - x)
    sp, sq = 16 - 12 * c, 4 + 12 * c
    yi = yh * 2 + kv
    oc = 1 - c

    core = (kv, ctx + 1 - 2 * c)

    def p_dev(d):
        return (kv, ctx + ((p + d) % 4 - p) * sp)

    def q_dev(d):
        return (kv, ctx + ((q + d) % 4 - q) * sq)

    def y_dev(d):
        to = (yi + d) % 4
        return (to % 2, ctx + (to // 2 - yh) * 2)

    far = (kv, ctx + 2 - 4 * yh)
    near_step = 3 - 2 * (yi % 2)
    near = y_dev(near_step)

    barrier = pltpu.get_barrier_semaphore()
    peers = [core] + [p_dev(d) for d in NEAR] + [q_dev(d) for d in NEAR] + [y_dev(d) for d in NEAR]
    for peer in peers:
        pl.semaphore_signal(barrier, inc=1, device_id=peer, device_id_type=MESH)

    def load(n, src, dst):
        copy = pltpu.make_async_copy(src, dst, ls.at[n])
        copy.start()
        return copy

    first = [load(0, ids_h, ids), load(1, q_h, qraw)]
    other_keys = load(2, ck_h.at[oc], kc.at[oc])
    other_values = load(3, cv_h.at[oc], vc.at[oc])
    own_keys = load(4, ck_h.at[c], kc.at[c])
    own_values = load(5, cv_h.at[c], vc.at[c])
    small = [
        load(6, mask_h, mask), load(7, dk_h, dk), load(8, dv_h, dv),
        load(9, res_h, rres.at[yh]), load(10, gain_h, gains.at[yh]),
    ]

    sent = []

    def send(src, dst, s_sem, r_sem, to):
        copy = pltpu.make_async_remote_copy(
            src_ref=src, dst_ref=dst, send_sem=s_sem, recv_sem=r_sem,
            device_id=to, device_id_type=MESH,
        )
        copy.start()
        sent.append((src, s_sem))

    def arrived(dst, sem):
        pltpu.make_async_copy(dst, dst, sem).wait()

    for copy in first:
        copy.wait()
    row = jnp.broadcast_to(ids[...].astype(f32), (64, 64))
    ii = lax.broadcasted_iota(i32, (64, 64), 0)
    jj = lax.broadcasted_iota(i32, (64, 64), 1)
    col = jnp.sum(jnp.where(ii == jj, row, 0.0), axis=1, keepdims=True)
    same = jnp.where(row == col, 1.0, 0.0)
    pos_col = jnp.sum(jnp.where(jj < ii, same, 0.0), axis=1, keepdims=True) + 32.0 * col
    pos_row = jnp.sum(jnp.where(ii < jj, same, 0.0), axis=0, keepdims=True) + 32.0 * row[:1]
    pt[...] = jnp.where(pos_col == jj.astype(f32), 1.0, 0.0).astype(bf16)
    pm[...] = jnp.where(pos_row == ii.astype(f32), 1.0, 0.0).astype(bf16)

    @pl.loop(0, 4)
    def _(n):
        at = pl.ds(mult(n * 1024, 1024), 1024)
        qs[:, at] = dot(pm[...], qraw[:, at]).astype(bf16)

    factor = HEAD ** (-0.5)
    c32, o32 = mult(c * 32, 32), mult(oc * 32, 32)
    first_slot = ctx * SLOTS

    def attend(t, t32, g):
        rows = jnp.concatenate(
            [qs[pl.ds(t32, 32), pl.ds(mult((g * 8 + k) * 128, 128), 128)] for k in range(8)], axis=0
        )
        at = pl.ds(mult(g * 128, 128), 128)
        s = dot(rows, kc[t, :, at], ((1,), (1,))) * factor
        live = lax.broadcasted_iota(i32, (1, SLOTS), 1) + first_slot < lens[t]
        s = jnp.where(live, s, NEG)
        m = jnp.max(s, axis=1, keepdims=True)
        e = jnp.where(live, jnp.exp(s - m), 0.0)
        l = jnp.sum(e, axis=1, keepdims=True)
        o = dot(e.astype(bf16), vc[t, :, at])
        some = l > 0.0
        safe = jnp.where(some, l, 1.0)
        o = o * (1.0 / safe)
        lse = jnp.where(some, m + jnp.log(safe), NEG)
        lane = lanes() % 32
        st = jnp.zeros((32, 128), f32)
        for k in range(8):
            st = jnp.where(lane == k, lse[k * 32 : (k + 1) * 32], st)
        return o, st

    other_keys.wait()
    other_values.wait()
    rest = [
        load(11, wo_h, wo), load(12, so_h, so), load(13, wg_h, wg), load(14, wu_h, wu),
        load(15, sg_h, sg), load(16, su_h, su), load(17, wd_h, wd), load(18, sd_h, sd),
    ]
    pl.semaphore_wait(barrier, len(peers))

    def offset(i):
        return 2 - i + 3 * (i // 2) - 2 * (i // 3)

    @pl.loop(0, 4)
    def _(i):
        d = offset(i)
        o, st = attend(oc, o32, (q + d) % 4)
        for k in range(8):
            acs[d, k] = o[k * 32 : (k + 1) * 32].astype(bf16)
        acs[d, 8] = split(st)
        pltpu.make_async_remote_copy(
            src_ref=acs.at[d], dst_ref=acr.at[d], send_sem=c_s.at[d], recv_sem=c_r.at[d],
            device_id=core, device_id_type=MESH,
        ).start()

    own_keys.wait()
    own_values.wait()
    for copy in small:
        copy.wait()
    send(rres.at[yh], rres.at[yh], r_s.at[0], r_r.at[0], near)
    send(gains.at[yh], gains.at[yh], r_s.at[1], r_r.at[1], near)

    @pl.loop(0, 4)
    def _(i):
        d = offset(i)
        o, st = attend(c, c32, (p + d) % 4)
        arrived(acr.at[d], c_r.at[d])
        factors, lse = blend([st, join(acr[d, 8])])
        for k in range(8):
            blocks = [o[k * 32 : (k + 1) * 32], acr[d, k].astype(f32)]
            a1s[d, k] = mixed_of(factors, blocks, k).astype(bf16)
        a1s[d, 8] = split(lse)

        @pl.when(d != 0)
        def _():
            pltpu.make_async_remote_copy(
                src_ref=a1s.at[d], dst_ref=a1r.at[d - 1], send_sem=a1_s.at[d - 1],
                recv_sem=a1_r.at[d - 1], device_id=p_dev(d), device_id_type=MESH,
            ).start()

    for d in range(4):
        sent.append((acs.at[d], c_s.at[d]))
    for d in ORDER:
        sent.append((a1s.at[d], a1_s.at[d - 1]))

    vis[...] = dot(pm[...], mask[...].astype(f32).astype(bf16))
    head0 = p * 8 + q * 2
    rows = jnp.concatenate(
        [qs[pl.ds(c32, 32), pl.ds(mult((head0 + k) * 128, 128), 128)] for k in range(2)], axis=0
    )
    at_p = pl.ds(mult(p * 128, 128), 128)
    seen = jnp.concatenate([vis[pl.ds(c32, 32), :]] * 2, axis=0) > 0.5
    s = jnp.where(seen, dot(rows, dk[:, at_p], ((1,), (1,))) * factor, NEG)
    m = jnp.max(s, axis=1, keepdims=True)
    e = jnp.where(seen, jnp.exp(s - m), 0.0)
    l = jnp.sum(e, axis=1, keepdims=True)
    draft_o = dot(e.astype(bf16), dv[:, at_p]) * (1.0 / l)
    lse = m + jnp.log(l)
    draft_st = jnp.where(lanes() % 32 == 0, lse[:32], lse[32:])

    for d in NEAR:
        arrived(a1r.at[d - 1], a1_r.at[d - 1])
    sources = [a1s.at[0]] + [a1r.at[n] for n in range(3)]
    factors, lse = blend([join(s[8]) for s in sources])
    keep = None
    for d in ORDER + (0,):
        to_q = (q + d) % 4
        shift = (128 - 2 * to_q) % 128
        turned = [pltpu.roll(f, shift, 1) for f in factors]
        heads = [
            mixed_of(turned, [s[2 * to_q + k].astype(f32) for s in sources], k) for k in range(2)
        ]
        st = pltpu.roll(lse, shift, 1)
        if d:
            a2s[d, 0] = heads[0].astype(bf16)
            a2s[d, 1] = heads[1].astype(bf16)
            a2s[d, 2] = split(st)
            send(a2s.at[d], a2r.at[d - 1], a2_s.at[d - 1], a2_r.at[d - 1], q_dev(d))
        else:
            keep = (heads, st)

    for d in NEAR:
        arrived(a2r.at[d - 1], a2_r.at[d - 1])
    factors, lse = blend([keep[1]] + [join(a2r[n, 2]) for n in range(3)])
    heads = [
        mixed_of(factors, [keep[0][k]] + [a2r[n, k].astype(f32) for n in range(3)], k)
        for k in range(2)
    ]
    a3s[0] = heads[0].astype(bf16)
    a3s[1] = heads[1].astype(bf16)
    a3s[2] = split(lse)
    send(a3s, a3r, a3_s.at[0], a3_r.at[0], far)
    arrived(a3r, a3_r.at[0])
    factors, _ = blend([lse, join(a3r[2]), draft_st])
    for k in range(2):
        blocks = [heads[k], a3r[k].astype(f32), draft_o[k * 32 : (k + 1) * 32]]
        ab[c, p, q, :, k * 128 : (k + 1) * 128] = mixed_of(factors, blocks, k).astype(bf16)

    def gather(buf, q_s, q_r, p_s, p_r, k_s, k_r, ring):
        def unit(dp, dq):
            return buf.at[c, (p - dp + 4) % 4, (q - dq + 4) % 4]

        def theirs(dp, dq):
            return buf.at[oc, (q - dp + 4) % 4, (p - dq + 4) % 4]

        def to_core(dp, dq):
            at = unit(dp, dq)
            send(at, at, k_s.at[dp, dq], k_r.at[dp, dq], core)

        def to_p(dq):
            at = unit(0, dq)
            for d in ORDER:
                send(at, at, p_s.at[d - 1, dq], p_r.at[d - 1, dq], p_dev(d))

        at = unit(0, 0)
        for d in ORDER:
            send(at, at, q_s.at[d - 1], q_r.at[d - 1], q_dev(d))
        to_p(0)
        to_core(0, 0)
        for dq in NEAR:
            arrived(unit(0, dq), q_r.at[dq - 1])
            to_p(dq)
            to_core(0, dq)

        def own_batch(dp):
            if dp:
                for dq in (0,) + NEAR:
                    arrived(unit(dp, dq), p_r.at[dp - 1, dq])
                    to_core(dp, dq)
            ring(c, (p - dp + 4) % 4, True)

        def core_batch(dp):
            for dq in (0,) + NEAR:
                arrived(theirs(dp, dq), k_r.at[dp, dq])
            ring(oc, (q - dp + 4) % 4, False)

        own_batch(0)
        own_batch(1)
        core_batch(0)
        own_batch(3)
        core_batch(1)
        own_batch(2)
        core_batch(3)
        core_batch(2)

    rest[0].wait()
    rest[1].wait()
    partial = {True: None, False: None}

    def out_batch(t, at_p, mine):
        lhs = jnp.concatenate([ab[t, at_p, n] for n in range(4)], axis=1)
        at = pl.ds(mult(at_p * 1024, 1024), 1024)
        both = jnp.concatenate([wo[at, :], so[t, at, :]], axis=1)
        value = dot(lhs, both)
        partial[mine] = value if partial[mine] is None else partial[mine] + value

    gather(ab, bq_s, bq_r, bp_s, bp_r, bc_s, bc_r, out_batch)
    for mine, t, t32 in ((True, c, c32), (False, oc, o32)):
        value = partial[mine]
        value = value[:, :128] + (dsc[t, 0] * D ** (-0.5)) * value[:, 128:]
        yb[yi, pl.ds(t32, 32), :] = value.astype(bf16)

    for d in ORDER:
        send(yb.at[yi], yb.at[yi], y_s.at[d - 1], y_r.at[d - 1], y_dev(d))
    arrived(rres.at[1 - yh], r_r.at[0])
    arrived(gains.at[1 - yh], r_r.at[1])
    base = [dot(pm[...], rres[b]) for b in range(2)]
    for d in NEAR:
        arrived(yb.at[(yi - d + 4) % 4], y_r.at[d - 1])
    squares = jnp.zeros((64, 1), f32)
    for b in range(2):
        h = base[b] + (yb[2 * b].astype(f32) + yb[2 * b + 1].astype(f32))
        hid[b] = h
        gb[c, p, q, :, b * 128 : (b + 1) * 128] = (h * gains[b]).astype(bf16)
        squares = squares + jnp.sum(h * h, axis=1, keepdims=True)
    ss[0, :, 0:64] = jnp.sum(jnp.where(ii == jj, squares, 0.0), axis=0, keepdims=True)
    ss[0, :, 64:128] = jnp.zeros((1, 64), f32)
    for d in ORDER:
        send(ss.at[0], ss.at[d], n_s.at[d - 1], n_r.at[d - 1], q_dev(d))

    for n in range(2, 6):
        rest[n].wait()
    sums = [None, None, None]

    def up_batch(t, at_p, mine):
        tp, tq = (sp, sq) if mine else (sq, sp)
        lhs = jnp.concatenate([gb[t, at_p, n] for n in range(4)], axis=1)

        def rows(ref, *lead):
            parts = []
            for n in range(4):
                start = (at_p * tp + n * tq + t) * 128
                for b in range(2):
                    parts.append(ref[(*lead, pl.ds(mult(start + b * 256, 128), 128), slice(None))])
            return jnp.concatenate(parts, axis=0)

        values = [dot(lhs, jnp.concatenate([rows(wg), rows(wu)], axis=1))]
        for n in range(2):
            both = jnp.concatenate([rows(sg, n), rows(su, n)], axis=1)
            values.append(dot(lhs[n * 32 : (n + 1) * 32], both))
        for n in range(3):
            sums[n] = values[n] if sums[n] is None else sums[n] + values[n]

    gather(gb, dq_s, dq_r, dp_s, dp_r, dc_s, dc_r, up_batch)
    for d in NEAR:
        arrived(ss.at[d], n_r.at[d - 1])
    ss[4] = ss[0] + ss[1] + ss[2] + ss[3]
    for d in ORDER:
        send(ss.at[4], ss.at[4 + d], n_s.at[2 + d], n_r.at[2 + d], p_dev(d))
    for d in NEAR:
        arrived(ss.at[4 + d], n_r.at[2 + d])
    ss[8] = ss[4] + ss[5] + ss[6] + ss[7]
    send(ss.at[8], ss.at[9], n_s.at[6], n_r.at[6], core)
    arrived(ss.at[9], n_r.at[6])
    whole = (ss[8] + ss[9])[:, 0:64]
    total = jnp.sum(jnp.where(ii == jj, whole, 0.0), axis=1, keepdims=True)
    scale = lax.rsqrt(total * (1.0 / D) + EPS)

    def halves(n, at):
        return dsc[0, n] * at, dsc[1, n] * at

    g0, g1 = halves(1, D ** (-0.5))
    u0, u1 = halves(2, D ** (-0.5))
    gate_delta = jnp.concatenate([g0 * sums[1][:, :128], g1 * sums[2][:, :128]], axis=0)
    up_delta = jnp.concatenate([u0 * sums[1][:, 128:], u1 * sums[2][:, 128:]], axis=0)
    gate = (sums[0][:, :128] + gate_delta) * scale
    up = (sums[0][:, 128:] + up_delta) * scale
    active = (gate / (1.0 + jnp.exp(-gate)) * up).astype(bf16)

    rest[6].wait()
    rest[7].wait()
    d0, d1 = halves(3, FF ** (-0.5))

    def down(t, at_p, tp, n, tq):
        start = (at_p * tp + n * tq + t) * 128

        def cols(ref, *lead):
            return jnp.concatenate(
                [
                    ref[(*lead, slice(None), pl.ds(mult(start + b * 256, 128), 128))]
                    for b in range(2)
                ],
                axis=1,
            )

        value = dot(active, cols(wd))
        delta = [d0 * dot(active[:32], cols(sd, 0)), d1 * dot(active[32:], cols(sd, 1))]
        return value + jnp.concatenate(delta, axis=0)

    for d in ORDER + (0,):
        for n in range(4):
            ecs[d, n] = down(oc, (q + d) % 4, sq, n, sp).astype(bf16)
        send(ecs.at[d], ecr.at[d], e0_s.at[d], e0_r.at[d], core)
    for d in ORDER + (0,):
        mine = [down(c, (p + d) % 4, sp, n, sq) for n in range(4)]
        arrived(ecr.at[d], e0_r.at[d])
        for n in range(4):
            value = mine[n] + ecr[d, n].astype(f32)
            if d:
                e1s[d - 1, n] = value.astype(bf16)
            else:
                e1o[n] = value
        if d:
            send(e1s.at[d - 1], e1r.at[d - 1], e1_s.at[d - 1], e1_r.at[d - 1], p_dev(d))
    for d in NEAR:
        arrived(e1r.at[d - 1], e1_r.at[d - 1])
    kept = None
    for d in ORDER + (0,):
        n = (q + d) % 4
        value = e1o[n]
        for s in range(3):
            value = value + e1r[s, n].astype(f32)
        if d:
            e2s[d - 1] = value.astype(bf16)
            send(e2s.at[d - 1], e2r.at[d - 1], e2_s.at[d - 1], e2_r.at[d - 1], q_dev(d))
        else:
            kept = value
    for d in NEAR:
        arrived(e2r.at[d - 1], e2_r.at[d - 1])
        kept = kept + e2r[d - 1].astype(f32)
    for b in range(2):
        e3s[b] = kept[:, b * 128 : (b + 1) * 128].astype(bf16)
    for d in ORDER:
        to_block = ((yi + d) % 4) // 2
        send(e3s.at[to_block], e3r.at[yi], e3_s.at[d - 1], e3_r.at[d - 1], y_dev(d))
    e3r[yi] = e3s[yh]
    for d in NEAR:
        arrived(e3r.at[(yi - d + 4) % 4], e3_r.at[d - 1])
    lowered = (e3r[0].astype(f32) + e3r[1].astype(f32)) + (e3r[2].astype(f32) + e3r[3].astype(f32))
    result = (hid[yh] + lowered).astype(bf16)
    out_ref[...] = dot(pt[...], result).astype(bf16)

    for src, sem in sent:
        pltpu.make_async_copy(src, src, sem).wait()


def shards(
    residual, queries, draft_keys, draft_values, cache_keys, cache_values, tenant_ids, tree_mask,
    cache_lengths, out_weight, out_signs, norm_gain, gate_weight, up_weight, down_weight,
    gate_signs, up_signs, down_signs, delta_scale,
):
    hbm = pl.BlockSpec(memory_space=pl.ANY)
    smem = pl.BlockSpec(memory_space=pltpu.SMEM)
    vm = pltpu.VMEM
    dma = pltpu.SemaphoreType.DMA
    scratch = [
        vm((1, 64), i32), vm((64, 64), i32), vm((64, 4096), bf16), vm((64, 4096), bf16),
        vm((2, SLOTS, 512), bf16), vm((2, SLOTS, 512), bf16), vm((64, 512), bf16),
        vm((64, 512), bf16), vm((64, 64), f32), vm((64, 64), bf16), vm((64, 64), bf16),
        vm((4096, 128), bf16), vm((2, 4096, 128), bf16), vm((8192, 128), bf16),
        vm((8192, 128), bf16), vm((128, 8192), bf16), vm((2, 8192, 128), bf16),
        vm((2, 8192, 128), bf16), vm((2, 128, 8192), bf16),
        vm((2, 64, 128), bf16), vm((2, 1, 128), f32),
        vm((4, 9, 32, 128), bf16), vm((4, 9, 32, 128), bf16),
        vm((4, 9, 32, 128), bf16), vm((3, 9, 32, 128), bf16),
        vm((4, 3, 32, 128), bf16), vm((3, 3, 32, 128), bf16),
        vm((3, 32, 128), bf16), vm((3, 32, 128), bf16),
        vm((2, 4, 4, 32, 256), bf16), vm((4, 64, 128), bf16), vm((2, 64, 128), f32),
        vm((2, 4, 4, 64, 256), bf16), vm((10, 1, 128), f32),
        vm((4, 4, 64, 256), bf16), vm((4, 4, 64, 256), bf16), vm((4, 64, 256), f32),
        vm((3, 4, 64, 256), bf16), vm((3, 4, 64, 256), bf16),
        vm((3, 64, 256), bf16), vm((3, 64, 256), bf16),
        vm((2, 64, 128), bf16), vm((4, 64, 128), bf16),
        dma((19,)), dma((4,)), dma((4,)), dma((3,)), dma((3,)), dma((3,)), dma((3,)),
        dma((1,)), dma((1,)), dma((2,)), dma((2,)),
        dma((3,)), dma((3,)), dma((3, 4)), dma((3, 4)), dma((4, 4)), dma((4, 4)),
        dma((3,)), dma((3,)),
        dma((3,)), dma((3,)), dma((3, 4)), dma((3, 4)), dma((4, 4)), dma((4, 4)),
        dma((7,)), dma((7,)),
        dma((4,)), dma((4,)), dma((3,)), dma((3,)), dma((3,)), dma((3,)), dma((3,)), dma((3,)),
    ]
    return pl.pallas_call(
        layer,
        name="layer",
        out_shape=jax.ShapeDtypeStruct((64, 128), bf16),
        in_specs=[hbm, hbm, smem, smem] + [hbm] * 15,
        out_specs=pl.BlockSpec(memory_space=pltpu.VMEM),
        scratch_shapes=scratch,
        compiler_params=pltpu.CompilerParams(
            collective_id=0, has_side_effects=True, vmem_limit_bytes=60 * 1024 * 1024
        ),
    )(
        tenant_ids.reshape(1, 64), tree_mask, cache_lengths, delta_scale, residual, queries,
        draft_keys, draft_values, cache_keys, cache_values, out_weight, out_signs,
        norm_gain.reshape(1, 128), gate_weight, up_weight, down_weight, gate_signs, up_signs,
        down_signs,
    )


def solution(mesh):
    return jax.shard_map(
        shards,
        mesh=mesh,
        in_specs=(
            P(None, "ctx"),
            P(None, "kv"),
            P(None, "kv"),
            P(None, "kv"),
            P(None, "ctx", "kv"),
            P(None, "ctx", "kv"),
            P(),
            P(),
            P(),
            P("kv", "ctx"),
            P(None, "kv", "ctx"),
            P("ctx"),
            P(None, ("kv", "ctx")),
            P(None, ("kv", "ctx")),
            P(("kv", "ctx"), None),
            P(None, None, ("kv", "ctx")),
            P(None, None, ("kv", "ctx")),
            P(None, ("kv", "ctx"), None),
            P(),
        ),
        out_specs=P(None, "ctx"),
        check_vma=False,
    )
```

time: 269 us -> 71.8 us (0.27)
  waiting for transfers between devices: 135 us -> 0 us
  Pallas kernels: 0 us -> 70.3 us
  starting transfers between devices: 42.8 us -> 0 us
  local copies, waits for them, and re-layouts: 27.9 us -> 1.32 us
  other arithmetic: 17.5 us -> 0 us
  matrix products: 16.8 us -> 0 us
  blocking collectives: 13.8 us -> 0 us
  between operations: 13.8 us -> 0.01 us
    all_to_all x6 -> x0, waiting for transfers between devices: 77.8 us -> none  [the longest x1 28.9 us: sent_together(): lax.all_to_all(both, axis, split_axis=split_dim, concat_axis=concat_dim,...]
    pallas_call x0 -> x1, Pallas kernels: none -> 70.3 us  [shards(): pl.pallas_call(layer, name='layer', out_shape=jax.ShapeDtypeStruct((64, 1...]
    all_gather x1 -> x0, waiting for transfers between devices: 57.7 us -> none  [shards(): piece = lax.all_gather(normed, 'ctx', axis=1, tiled=True)]
    all_to_all x6 -> x0, starting transfers between devices: 42.8 us -> none  [the longest x3 12.1 us: sent_to_all(): return lax.all_to_all(copies, axis, split_axis=0, concat_axis=0, tiled=True)]
    dot_general x14 -> x0, matrix products: 16.8 us -> none  [the longest x1 3.98 us: shards(): jnp.einsum('tqgwd,tjgd->tqgwj', query_blocks, cache_key_blocks, preferred...]
    all_to_all x1 -> x0, blocking collectives: 13.8 us -> none  [sent_to_all(): return lax.all_to_all(copies, axis, split_axis=0, concat_axis=0, tiled=True)]
    reduce_sum x9 -> x0, other arithmetic: 7.99 us -> none  [the longest x1 3.53 us: shards(): total = jnp.sum(weights, axis=-1)]
    reshape x4 -> x0, local copies, waits for them, and re-layouts: 6.11 us -> none  [the longest x1 2.15 us: shards(): cache_keys.reshape(tenants, ctx_rows, groups_here, HEAD_SIZE)]
  transfers between devices with their start and end apart: 7 -> 0, of which waited for: 6 -> 0; matrix products, arithmetic and copies ran while one was open for 9% -> 0% of each run, Pallas kernels for 0% -> 0%
where the time goes in v1:
time: 71.8 us; the launch traced here: 71.6 us
  Pallas kernels  70.3 us (98%)
  local copies, waits for them, and re-layouts  1.32 us (2%)
    pallas_call x1, Pallas kernels, shards(): pl.pallas_call(layer, name='layer', out_shape=jax.ShapeDtypeStruct((64, 1...  70.3 us

profile of v1, /device:TPU:0, one launch (start us, length us, event | category | flops | bytes accessed | tf_op | source)
XLA Modules:
  0.0 71.6 jit_solution(7082815370008774287)
XLA Ops:
  0.0 70.3 %layer.1 = bf16[64,128]{1,0:T(8,128)(2,1)} custom-call(s32[1,64]{1,0:T(1,128)} %bitcast.2, s32[64,64]{1,0:T(8,128)} %mask_h.1, s32[2]{0:T(128)} %lens.1, f32[2,4]{1,0:T(2,128)} %dsc.1, bf16[64,128]{1,0:T(8,128)(2,1)} %res_h.1, bf16[64,4096]{1,0:T(8,128)(2,1)} %q_h.1, bf16[64,512]{1,0:T(8,128)(2,1)} %dk_h.1, bf16[64,512]{1,0:T(8,128)(2,1)} %dv_h.1, ...), custom_call_target="tpu_custom_call" | custom-call | tf_op jit(solution)/shard_map/layer/pallas_call | solution.py:517
  70.3 1.3 %copy.21 = bf16[64,128]{1,0:T(8,128)(2,1)} copy(bf16[64,128]{1,0:T(8,128)(2,1)} %layer.1) | data formatting | bytes 32768

commit v2 on v1

--- a/solution.py
+++ b/solution.py
@@ -12,6 +12,7 @@
 HEAD = 128
 SLOTS = 512
 NEG = -1e30
+LOG2E = 1.4426950408889634
 EPS = 1e-05
 MESH = pl.DeviceIdType.MESH
 f32, bf16, i32 = jnp.float32, jnp.bfloat16, jnp.int32
@@ -65,9 +66,9 @@
     wg_h, wu_h, wd_h, sg_h, su_h, sd_h,
     out_ref,
     ids, mask, qraw, qs, kc, vc, dk, dv, vis, pm, pt, wo, so, wg, wu, wd, sg, su, sd,
-    rres, gains, acs, acr, a1s, a1r, a2s, a2r, a3s, a3r, ab, yb, hid, gb, ss,
+    rres, gains, acs, acr, a1s, a1r, a2s, a2r, ab, yb, hid, gb, ss,
     ecs, ecr, e1o, e1s, e1r, e2s, e2r, e3s, e3r,
-    ls, c_s, c_r, a1_s, a1_r, a2_s, a2_r, a3_s, a3_r, r_s, r_r,
+    ls, c_s, c_r, a1_s, a1_r, a2_s, a2_r, r_s, r_r,
     bq_s, bq_r, bp_s, bp_r, bc_s, bc_r, y_s, y_r,
     dq_s, dq_r, dp_s, dp_r, dc_s, dc_r, n_s, n_r,
     e0_s, e0_r, e1_s, e1_r, e2_s, e2_r, e3_s, e3_r,
@@ -95,21 +96,23 @@
         to = (yi + d) % 4
         return (to % 2, ctx + (to // 2 - yh) * 2)
 
-    far = (kv, ctx + 2 - 4 * yh)
+    def qy_dev(d, e):
+        return (kv, q_dev(d)[1] + e * (2 - 4 * yh))
+
     near_step = 3 - 2 * (yi % 2)
     near = y_dev(near_step)
 
     barrier = pltpu.get_barrier_semaphore()
     peers = [core] + [p_dev(d) for d in NEAR] + [q_dev(d) for d in NEAR] + [y_dev(d) for d in NEAR]
-    for peer in peers:
-        pl.semaphore_signal(barrier, inc=1, device_id=peer, device_id_type=MESH)
-
+    peers += [qy_dev(d, 1) for d in NEAR]
     def load(n, src, dst):
         copy = pltpu.make_async_copy(src, dst, ls.at[n])
         copy.start()
         return copy
 
     first = [load(0, ids_h, ids), load(1, q_h, qraw)]
+    for peer in peers:
+        pl.semaphore_signal(barrier, inc=1, device_id=peer, device_id_type=MESH)
     other_keys = load(2, ck_h.at[oc], kc.at[oc])
     other_values = load(3, cv_h.at[oc], vc.at[oc])
     own_keys = load(4, ck_h.at[c], kc.at[c])
@@ -158,17 +161,18 @@
             [qs[pl.ds(t32, 32), pl.ds(mult((g * 8 + k) * 128, 128), 128)] for k in range(8)], axis=0
         )
         at = pl.ds(mult(g * 128, 128), 128)
-        s = dot(rows, kc[t, :, at], ((1,), (1,))) * factor
+        s = dot(rows, kc[t, :, at], ((1,), (1,)))
         live = lax.broadcasted_iota(i32, (1, SLOTS), 1) + first_slot < lens[t]
         s = jnp.where(live, s, NEG)
         m = jnp.max(s, axis=1, keepdims=True)
-        e = jnp.where(live, jnp.exp(s - m), 0.0)
+        m = jnp.where(m > 0.5 * NEG, m, 0.0)
+        e = jnp.exp2((s - m) * (factor * LOG2E))
         l = jnp.sum(e, axis=1, keepdims=True)
         o = dot(e.astype(bf16), vc[t, :, at])
         some = l > 0.0
         safe = jnp.where(some, l, 1.0)
         o = o * (1.0 / safe)
-        lse = jnp.where(some, m + jnp.log(safe), NEG)
+        lse = jnp.where(some, m * factor + jnp.log(safe), NEG)
         lane = lanes() % 32
         st = jnp.zeros((32, 128), f32)
         for k in range(8):
@@ -181,22 +185,30 @@
         load(11, wo_h, wo), load(12, so_h, so), load(13, wg_h, wg), load(14, wu_h, wu),
         load(15, sg_h, sg), load(16, su_h, su), load(17, wd_h, wd), load(18, sd_h, sd),
     ]
-    pl.semaphore_wait(barrier, len(peers))
-
     def offset(i):
         return 2 - i + 3 * (i // 2) - 2 * (i // 3)
 
-    @pl.loop(0, 4)
-    def _(i):
-        d = offset(i)
+    def other_block(d):
         o, st = attend(oc, o32, (q + d) % 4)
         for k in range(8):
             acs[d, k] = o[k * 32 : (k + 1) * 32].astype(bf16)
         acs[d, 8] = split(st)
+
+    def other_send(d):
         pltpu.make_async_remote_copy(
             src_ref=acs.at[d], dst_ref=acr.at[d], send_sem=c_s.at[d], recv_sem=c_r.at[d],
             device_id=core, device_id_type=MESH,
         ).start()
+
+    other_block(2)
+    pl.semaphore_wait(barrier, len(peers))
+    other_send(2)
+
+    @pl.loop(1, 4)
+    def _(i):
+        d = offset(i)
+        other_block(d)
+        other_send(d)
 
     own_keys.wait()
     own_values.wait()
@@ -256,32 +268,28 @@
             mixed_of(turned, [s[2 * to_q + k].astype(f32) for s in sources], k) for k in range(2)
         ]
         st = pltpu.roll(lse, shift, 1)
-        if d:
-            a2s[d, 0] = heads[0].astype(bf16)
-            a2s[d, 1] = heads[1].astype(bf16)
-            a2s[d, 2] = split(st)
-            send(a2s.at[d], a2r.at[d - 1], a2_s.at[d - 1], a2_r.at[d - 1], q_dev(d))
-        else:
+        a2s[d, 0] = heads[0].astype(bf16)
+        a2s[d, 1] = heads[1].astype(bf16)
+        a2s[d, 2] = split(st)
+        for e in (1, 0):
+            if d or e:
+                send(a2s.at[d], a2r.at[e, d], a2_s.at[e, d], a2_r.at[e, d], qy_dev(d, e))
+        if not d:
             keep = (heads, st)
 
-    for d in NEAR:
-        arrived(a2r.at[d - 1], a2_r.at[d - 1])
-    factors, lse = blend([keep[1]] + [join(a2r[n, 2]) for n in range(3)])
-    heads = [
-        mixed_of(factors, [keep[0][k]] + [a2r[n, k].astype(f32) for n in range(3)], k)
-        for k in range(2)
-    ]
-    a3s[0] = heads[0].astype(bf16)
-    a3s[1] = heads[1].astype(bf16)
-    a3s[2] = split(lse)
-    send(a3s, a3r, a3_s.at[0], a3_r.at[0], far)
-    arrived(a3r, a3_r.at[0])
-    factors, _ = blend([lse, join(a3r[2]), draft_st])
+    others = [(0, 1), (0, 3), (1, 0), (1, 1), (1, 3), (0, 2), (1, 2)]
+    for e, d in others:
+        arrived(a2r.at[e, d], a2_r.at[e, d])
+    factors, _ = blend([keep[1]] + [join(a2r[e, d, 2]) for e, d in others] + [draft_st])
     for k in range(2):
-        blocks = [heads[k], a3r[k].astype(f32), draft_o[k * 32 : (k + 1) * 32]]
+        blocks = [keep[0][k]] + [a2r[e, d, k].astype(f32) for e, d in others]
+        blocks.append(draft_o[k * 32 : (k + 1) * 32])
         ab[c, p, q, :, k * 128 : (k + 1) * 128] = mixed_of(factors, blocks, k).astype(bf16)
 
-    def gather(buf, q_s, q_r, p_s, p_r, k_s, k_r, ring):
+    def nothing():
+        pass
+
+    def gather(buf, q_s, q_r, p_s, p_r, k_s, k_r, ring, after_q=nothing, after_p=nothing):
         def unit(dp, dq):
             return buf.at[c, (p - dp + 4) % 4, (q - dq + 4) % 4]
 
@@ -306,6 +314,7 @@
             arrived(unit(0, dq), q_r.at[dq - 1])
             to_p(dq)
             to_core(0, dq)
+        after_q()
 
         def own_batch(dp):
             if dp:
@@ -325,6 +334,7 @@
         own_batch(3)
         core_batch(1)
         own_batch(2)
+        after_p()
         core_batch(3)
         core_batch(2)
 
@@ -386,16 +396,20 @@
         for n in range(3):
             sums[n] = values[n] if sums[n] is None else sums[n] + values[n]
 
-    gather(gb, dq_s, dq_r, dp_s, dp_r, dc_s, dc_r, up_batch)
-    for d in NEAR:
-        arrived(ss.at[d], n_r.at[d - 1])
-    ss[4] = ss[0] + ss[1] + ss[2] + ss[3]
-    for d in ORDER:
-        send(ss.at[4], ss.at[4 + d], n_s.at[2 + d], n_r.at[2 + d], p_dev(d))
-    for d in NEAR:
-        arrived(ss.at[4 + d], n_r.at[2 + d])
-    ss[8] = ss[4] + ss[5] + ss[6] + ss[7]
-    send(ss.at[8], ss.at[9], n_s.at[6], n_r.at[6], core)
+    def squares_q():
+        for d in NEAR:
+            arrived(ss.at[d], n_r.at[d - 1])
+        ss[4] = ss[0] + ss[1] + ss[2] + ss[3]
+        for d in ORDER:
+            send(ss.at[4], ss.at[4 + d], n_s.at[2 + d], n_r.at[2 + d], p_dev(d))
+
+    def squares_p():
+        for d in NEAR:
+            arrived(ss.at[4 + d], n_r.at[2 + d])
+        ss[8] = ss[4] + ss[5] + ss[6] + ss[7]
+        send(ss.at[8], ss.at[9], n_s.at[6], n_r.at[6], core)
+
+    gather(gb, dq_s, dq_r, dp_s, dp_r, dc_s, dc_r, up_batch, squares_q, squares_p)
     arrived(ss.at[9], n_r.at[6])
     whole = (ss[8] + ss[9])[:, 0:64]
     total = jnp.sum(jnp.where(ii == jj, whole, 0.0), axis=1, keepdims=True)
@@ -432,11 +446,12 @@
         delta = [d0 * dot(active[:32], cols(sd, 0)), d1 * dot(active[32:], cols(sd, 1))]
         return value + jnp.concatenate(delta, axis=0)
 
-    for d in ORDER + (0,):
+    def down_other(d):
         for n in range(4):
             ecs[d, n] = down(oc, (q + d) % 4, sq, n, sp).astype(bf16)
         send(ecs.at[d], ecr.at[d], e0_s.at[d], e0_r.at[d], core)
-    for d in ORDER + (0,):
+
+    def down_own(d):
         mine = [down(c, (p + d) % 4, sp, n, sq) for n in range(4)]
         arrived(ecr.at[d], e0_r.at[d])
         for n in range(4):
@@ -447,6 +462,15 @@
                 e1o[n] = value
         if d:
             send(e1s.at[d - 1], e1r.at[d - 1], e1_s.at[d - 1], e1_r.at[d - 1], p_dev(d))
+
+    down_other(2)
+    down_other(1)
+    down_other(3)
+    down_own(2)
+    down_other(0)
+    down_own(1)
+    down_own(3)
+    down_own(0)
     for d in NEAR:
         arrived(e1r.at[d - 1], e1_r.at[d - 1])
     kept = None
@@ -484,7 +508,7 @@
     cache_lengths, out_weight, out_signs, norm_gain, gate_weight, up_weight, down_weight,
     gate_signs, up_signs, down_signs, delta_scale,
 ):
-    hbm = pl.BlockSpec(memory_space=pl.ANY)
+    hbm = pl.BlockSpec(memory_space=pltpu.HBM)
     smem = pl.BlockSpec(memory_space=pltpu.SMEM)
     vm = pltpu.VMEM
     dma = pltpu.SemaphoreType.DMA
@@ -498,16 +522,15 @@
         vm((2, 64, 128), bf16), vm((2, 1, 128), f32),
         vm((4, 9, 32, 128), bf16), vm((4, 9, 32, 128), bf16),
         vm((4, 9, 32, 128), bf16), vm((3, 9, 32, 128), bf16),
-        vm((4, 3, 32, 128), bf16), vm((3, 3, 32, 128), bf16),
-        vm((3, 32, 128), bf16), vm((3, 32, 128), bf16),
+        vm((4, 3, 32, 128), bf16), vm((2, 4, 3, 32, 128), bf16),
         vm((2, 4, 4, 32, 256), bf16), vm((4, 64, 128), bf16), vm((2, 64, 128), f32),
         vm((2, 4, 4, 64, 256), bf16), vm((10, 1, 128), f32),
         vm((4, 4, 64, 256), bf16), vm((4, 4, 64, 256), bf16), vm((4, 64, 256), f32),
         vm((3, 4, 64, 256), bf16), vm((3, 4, 64, 256), bf16),
         vm((3, 64, 256), bf16), vm((3, 64, 256), bf16),
         vm((2, 64, 128), bf16), vm((4, 64, 128), bf16),
-        dma((19,)), dma((4,)), dma((4,)), dma((3,)), dma((3,)), dma((3,)), dma((3,)),
-        dma((1,)), dma((1,)), dma((2,)), dma((2,)),
+        dma((19,)), dma((4,)), dma((4,)), dma((3,)), dma((3,)), dma((2, 4)), dma((2, 4)),
+        dma((2,)), dma((2,)),
         dma((3,)), dma((3,)), dma((3, 4)), dma((3, 4)), dma((4, 4)), dma((4, 4)),
         dma((3,)), dma((3,)),
         dma((3,)), dma((3,)), dma((3, 4)), dma((3, 4)), dma((4, 4)), dma((4, 4)),
@@ -517,7 +540,7 @@
     return pl.pallas_call(
         layer,
         name="layer",
-        out_shape=jax.ShapeDtypeStruct((64, 128), bf16),
+        out_shape=pltpu.VMEM((64, 128), bf16),
         in_specs=[hbm, hbm, smem, smem] + [hbm] * 15,
         out_specs=pl.BlockSpec(memory_space=pltpu.VMEM),
         scratch_shapes=scratch,

time: 71.8 us -> 63.6 us (0.89)
  Pallas kernels: 70.3 us -> 62.9 us
    pallas_call x1, Pallas kernels: 70.3 us -> 62.9 us  [shards(): pl.pallas_call(layer, name='layer', out_shape=pltpu.VMEM((64, 128), bf16)...]
where the time goes in v2:
time: 63.6 us; the launch traced here: 63.5 us
  Pallas kernels  62.9 us (99%)
    pallas_call x1, Pallas kernels, shards(): pl.pallas_call(layer, name='layer', out_shape=pltpu.VMEM((64, 128), bf16)...  62.9 us

profile of v2, /device:TPU:0, one launch (start us, length us, event | category | flops | bytes accessed | tf_op | source)
XLA Modules:
  0.0 63.5 jit_solution(10622342817392506916)
XLA Ops:
  0.0 62.9 %layer.1 = bf16[64,128]{1,0:T(8,128)(2,1)S(1)} custom-call(s32[1,64]{1,0:T(1,128)} %bitcast.2, s32[64,64]{1,0:T(8,128)} %mask_h.1, s32[2]{0:T(128)} %lens.1, f32[2,4]{1,0:T(2,128)} %dsc.1, bf16[64,128]{1,0:T(8,128)(2,1)} %res_h.1, bf16[64,4096]{1,0:T(8,128)(2,1)} %q_h.1, bf16[64,512]{1,0:T(8,128)(2,1)} %dk_h.1, bf16[64,512]{1,0:T(8,128)(2,1)} %dv_h.1, ...), custom_call_target="tpu_custom_call" | custom-call | tf_op jit(solution)/shard_map/layer/pallas_call | solution.py:540
  62.9 0.6 copy.21

commit v3 on v2

--- a/solution.py
+++ b/solution.py
@@ -62,16 +62,13 @@
 
 
 def layer(
-    ids_h, mask_h, lens, dsc, res_h, q_h, dk_h, dv_h, ck_h, cv_h, wo_h, so_h, gain_h,
+    ids_h, mask_h, lens_h, dsc_h, res_h, q_h, dk_h, dv_h, ck_h, cv_h, wo_h, so_h, gain_h,
     wg_h, wu_h, wd_h, sg_h, su_h, sd_h,
     out_ref,
-    ids, mask, qraw, qs, kc, vc, dk, dv, vis, pm, pt, wo, so, wg, wu, wd, sg, su, sd,
+    lens, dsc, ids, mask, qraw, qs, kc, vc, dk, dv, vis, pm, pt, wo, so, wg, wu, wd, sg, su, sd,
     rres, gains, acs, acr, a1s, a1r, a2s, a2r, ab, yb, hid, gb, ss,
-    ecs, ecr, e1o, e1s, e1r, e2s, e2r, e3s, e3r,
-    ls, c_s, c_r, a1_s, a1_r, a2_s, a2_r, r_s, r_r,
-    bq_s, bq_r, bp_s, bp_r, bc_s, bc_r, y_s, y_r,
-    dq_s, dq_r, dp_s, dp_r, dc_s, dc_r, n_s, n_r,
-    e0_s, e0_r, e1_s, e1_r, e2_s, e2_r, e3_s, e3_r,
+    ecs, ecr, e1o, e1s, e1r, e3s, e3r,
+    ls, sem_s, c_r, a1_r, a2_r, r_r, bq_r, bp_r, bc_r, y_r, dq_r, dp_r, dc_r, n_r, e0_r, e1_r, e3_r,
 ):
     kv, ctx = lax.axis_index("kv"), lax.axis_index("ctx")
     c = ctx % 2
@@ -96,6 +93,9 @@
         to = (yi + d) % 4
         return (to % 2, ctx + (to // 2 - yh) * 2)
 
+    def pq_dev(d, e):
+        return (kv, p_dev(d)[1] + q_dev(e)[1] - ctx)
+
     def qy_dev(d, e):
         return (kv, q_dev(d)[1] + e * (2 - 4 * yh))
 
@@ -105,32 +105,36 @@
     barrier = pltpu.get_barrier_semaphore()
     peers = [core] + [p_dev(d) for d in NEAR] + [q_dev(d) for d in NEAR] + [y_dev(d) for d in NEAR]
     peers += [qy_dev(d, 1) for d in NEAR]
+    peers += [pq_dev(d, e) for d in NEAR for e in NEAR]
     def load(n, src, dst):
         copy = pltpu.make_async_copy(src, dst, ls.at[n])
         copy.start()
         return copy
 
-    first = [load(0, ids_h, ids), load(1, q_h, qraw)]
+    first = [load(0, ids_h, ids), load(1, q_h, qraw), load(17, lens_h, lens), load(18, dsc_h, dsc)]
     for peer in peers:
         pl.semaphore_signal(barrier, inc=1, device_id=peer, device_id_type=MESH)
-    other_keys = load(2, ck_h.at[oc], kc.at[oc])
-    other_values = load(3, cv_h.at[oc], vc.at[oc])
-    own_keys = load(4, ck_h.at[c], kc.at[c])
-    own_values = load(5, cv_h.at[c], vc.at[c])
+    load(2, ck_h.at[oc], kc.at[oc])
+    load(2, cv_h.at[oc], vc.at[oc])
+    load(3, ck_h.at[c], kc.at[c])
+    load(3, cv_h.at[c], vc.at[c])
     small = [
-        load(6, mask_h, mask), load(7, dk_h, dk), load(8, dv_h, dv),
-        load(9, res_h, rres.at[yh]), load(10, gain_h, gains.at[yh]),
+        load(4, mask_h, mask), load(5, dk_h, dk), load(6, dv_h, dv),
+        load(7, res_h, rres.at[yh]), load(8, gain_h, gains.at[yh]),
     ]
 
-    sent = []
-
-    def send(src, dst, s_sem, r_sem, to):
-        copy = pltpu.make_async_remote_copy(
-            src_ref=src, dst_ref=dst, send_sem=s_sem, recv_sem=r_sem,
+    big, tiny = [0], [0]
+
+    def send(src, dst, r_sem, to):
+        size = 1
+        for n in src.shape:
+            size *= n
+        small_one = src.dtype == f32
+        (tiny if small_one else big)[0] += size * (4 if small_one else 2)
+        pltpu.make_async_remote_copy(
+            src_ref=src, dst_ref=dst, send_sem=sem_s.at[1 if small_one else 0], recv_sem=r_sem,
             device_id=to, device_id_type=MESH,
-        )
-        copy.start()
-        sent.append((src, s_sem))
+        ).start()
 
     def arrived(dst, sem):
         pltpu.make_async_copy(dst, dst, sem).wait()
@@ -147,9 +151,8 @@
     pt[...] = jnp.where(pos_col == jj.astype(f32), 1.0, 0.0).astype(bf16)
     pm[...] = jnp.where(pos_row == ii.astype(f32), 1.0, 0.0).astype(bf16)
 
-    @pl.loop(0, 4)
-    def _(n):
-        at = pl.ds(mult(n * 1024, 1024), 1024)
+    for n in range(4):
+        at = pl.ds(n * 1024, 1024)
         qs[:, at] = dot(pm[...], qraw[:, at]).astype(bf16)
 
     factor = HEAD ** (-0.5)
@@ -179,15 +182,11 @@
             st = jnp.where(lane == k, lse[k * 32 : (k + 1) * 32], st)
         return o, st
 
-    other_keys.wait()
-    other_values.wait()
+    arrived(kc, ls.at[2])
     rest = [
-        load(11, wo_h, wo), load(12, so_h, so), load(13, wg_h, wg), load(14, wu_h, wu),
-        load(15, sg_h, sg), load(16, su_h, su), load(17, wd_h, wd), load(18, sd_h, sd),
+        load(9, wo_h, wo), load(10, so_h, so), load(11, wg_h, wg), load(12, wu_h, wu),
+        load(13, sg_h, sg), load(14, su_h, su), load(15, wd_h, wd), load(16, sd_h, sd),
     ]
-    def offset(i):
-        return 2 - i + 3 * (i // 2) - 2 * (i // 3)
-
     def other_block(d):
         o, st = attend(oc, o32, (q + d) % 4)
         for k in range(8):
@@ -195,50 +194,37 @@
         acs[d, 8] = split(st)
 
     def other_send(d):
-        pltpu.make_async_remote_copy(
-            src_ref=acs.at[d], dst_ref=acr.at[d], send_sem=c_s.at[d], recv_sem=c_r.at[d],
-            device_id=core, device_id_type=MESH,
-        ).start()
-
-    other_block(2)
+        send(acs.at[d], acr.at[d], c_r.at[d], core)
+
+    for d in ORDER + (0,):
+        other_block(d)
     pl.semaphore_wait(barrier, len(peers))
-    other_send(2)
-
-    @pl.loop(1, 4)
-    def _(i):
-        d = offset(i)
-        other_block(d)
+    for d in ORDER + (0,):
         other_send(d)
 
-    own_keys.wait()
-    own_values.wait()
+    arrived(kc, ls.at[3])
     for copy in small:
         copy.wait()
-    send(rres.at[yh], rres.at[yh], r_s.at[0], r_r.at[0], near)
-    send(gains.at[yh], gains.at[yh], r_s.at[1], r_r.at[1], near)
-
-    @pl.loop(0, 4)
-    def _(i):
-        d = offset(i)
-        o, st = attend(c, c32, (p + d) % 4)
-        arrived(acr.at[d], c_r.at[d])
+    send(rres.at[yh], rres.at[yh], r_r.at[0], near)
+    send(gains.at[yh], gains.at[yh], r_r.at[1], near)
+
+    def merge(d, o, st):
         factors, lse = blend([st, join(acr[d, 8])])
         for k in range(8):
             blocks = [o[k * 32 : (k + 1) * 32], acr[d, k].astype(f32)]
             a1s[d, k] = mixed_of(factors, blocks, k).astype(bf16)
         a1s[d, 8] = split(lse)
-
-        @pl.when(d != 0)
-        def _():
-            pltpu.make_async_remote_copy(
-                src_ref=a1s.at[d], dst_ref=a1r.at[d - 1], send_sem=a1_s.at[d - 1],
-                recv_sem=a1_r.at[d - 1], device_id=p_dev(d), device_id_type=MESH,
-            ).start()
-
-    for d in range(4):
-        sent.append((acs.at[d], c_s.at[d]))
-    for d in ORDER:
-        sent.append((a1s.at[d], a1_s.at[d - 1]))
+        if d:
+            send(a1s.at[d], a1r.at[d - 1], a1_r.at[0], p_dev(d))
+
+    pending = []
+    for d in ORDER + (0,):
+        pending.append((d, *attend(c, c32, (p + d) % 4)))
+        if len(pending) > 1:
+            arrived(acr.at[pending[0][0]], c_r.at[pending[0][0]])
+            merge(*pending.pop(0))
+    arrived(acr.at[0], c_r.at[0])
+    merge(*pending.pop(0))
 
     vis[...] = dot(pm[...], mask[...].astype(f32).astype(bf16))
     head0 = p * 8 + q * 2
@@ -255,8 +241,7 @@
     lse = m + jnp.log(l)
     draft_st = jnp.where(lanes() % 32 == 0, lse[:32], lse[32:])
 
-    for d in NEAR:
-        arrived(a1r.at[d - 1], a1_r.at[d - 1])
+    arrived(a1r, a1_r.at[0])
     sources = [a1s.at[0]] + [a1r.at[n] for n in range(3)]
     factors, lse = blend([join(s[8]) for s in sources])
     keep = None
@@ -273,68 +258,67 @@
         a2s[d, 2] = split(st)
         for e in (1, 0):
             if d or e:
-                send(a2s.at[d], a2r.at[e, d], a2_s.at[e, d], a2_r.at[e, d], qy_dev(d, e))
+                send(a2s.at[d], a2r.at[4 * e + d], a2_r.at[0], qy_dev(d, e))
         if not d:
             keep = (heads, st)
 
     others = [(0, 1), (0, 3), (1, 0), (1, 1), (1, 3), (0, 2), (1, 2)]
-    for e, d in others:
-        arrived(a2r.at[e, d], a2_r.at[e, d])
-    factors, _ = blend([keep[1]] + [join(a2r[e, d, 2]) for e, d in others] + [draft_st])
+    arrived(a2r.at[pl.ds(1, 7)], a2_r.at[0])
+    factors, _ = blend([keep[1]] + [join(a2r[4 * e + d, 2]) for e, d in others] + [draft_st])
     for k in range(2):
-        blocks = [keep[0][k]] + [a2r[e, d, k].astype(f32) for e, d in others]
+        blocks = [keep[0][k]] + [a2r[4 * e + d, k].astype(f32) for e, d in others]
         blocks.append(draft_o[k * 32 : (k + 1) * 32])
         ab[c, p, q, :, k * 128 : (k + 1) * 128] = mixed_of(factors, blocks, k).astype(bf16)
 
     def nothing():
         pass
 
-    def gather(buf, q_s, q_r, p_s, p_r, k_s, k_r, ring, after_q=nothing, after_p=nothing):
-        def unit(dp, dq):
-            return buf.at[c, (p - dp + 4) % 4, (q - dq + 4) % 4]
-
-        def theirs(dp, dq):
-            return buf.at[oc, (q - dp + 4) % 4, (p - dq + 4) % 4]
-
-        def to_core(dp, dq):
-            at = unit(dp, dq)
-            send(at, at, k_s.at[dp, dq], k_r.at[dp, dq], core)
-
-        def to_p(dq):
-            at = unit(0, dq)
+    def gather(buf, direct, q_r, p_r, k_r, ring, after_q=nothing, after_p=nothing):
+        mine = buf.at[c, p, q]
+
+        def row_of(dp):
+            return buf.at[c, (p - dp + 4) % 4]
+
+        def to_core(dp):
+            send(row_of(dp), row_of(dp), k_r.at[dp], core)
+
+        if direct:
+            for dp in (0,) + ORDER:
+                for dq in ORDER + (0,):
+                    if dp or dq:
+                        send(mine, mine, p_r.at[dp], pq_dev(dp, dq))
+            arrived(buf.at[c, p, pl.ds(0, 3)], p_r.at[0])
+        else:
             for d in ORDER:
-                send(at, at, p_s.at[d - 1, dq], p_r.at[d - 1, dq], p_dev(d))
-
-        at = unit(0, 0)
-        for d in ORDER:
-            send(at, at, q_s.at[d - 1], q_r.at[d - 1], q_dev(d))
-        to_p(0)
-        to_core(0, 0)
-        for dq in NEAR:
-            arrived(unit(0, dq), q_r.at[dq - 1])
-            to_p(dq)
-            to_core(0, dq)
+                send(mine, mine, q_r.at[d - 1], q_dev(d))
+            for d in ORDER:
+                send(mine, mine, p_r.at[d], p_dev(d))
+            for dq in NEAR:
+                at = buf.at[c, p, (q - dq + 4) % 4]
+                arrived(at, q_r.at[dq - 1])
+                for d in ORDER:
+                    send(at, at, p_r.at[d], p_dev(d))
+        to_core(0)
         after_q()
 
         def own_batch(dp):
             if dp:
-                for dq in (0,) + NEAR:
-                    arrived(unit(dp, dq), p_r.at[dp - 1, dq])
-                    to_core(dp, dq)
+                arrived(row_of(dp), p_r.at[dp])
+                to_core(dp)
             ring(c, (p - dp + 4) % 4, True)
 
         def core_batch(dp):
-            for dq in (0,) + NEAR:
-                arrived(theirs(dp, dq), k_r.at[dp, dq])
-            ring(oc, (q - dp + 4) % 4, False)
+            at_p = (q - dp + 4) % 4
+            arrived(buf.at[oc, at_p], k_r.at[dp])
+            ring(oc, at_p, False)
 
         own_batch(0)
         own_batch(1)
+        own_batch(3)
         core_batch(0)
-        own_batch(3)
-        core_batch(1)
         own_batch(2)
         after_p()
+        core_batch(1)
         core_batch(3)
         core_batch(2)
 
@@ -349,19 +333,18 @@
         value = dot(lhs, both)
         partial[mine] = value if partial[mine] is None else partial[mine] + value
 
-    gather(ab, bq_s, bq_r, bp_s, bp_r, bc_s, bc_r, out_batch)
+    gather(ab, True, bq_r, bp_r, bc_r, out_batch)
     for mine, t, t32 in ((True, c, c32), (False, oc, o32)):
         value = partial[mine]
         value = value[:, :128] + (dsc[t, 0] * D ** (-0.5)) * value[:, 128:]
         yb[yi, pl.ds(t32, 32), :] = value.astype(bf16)
 
     for d in ORDER:
-        send(yb.at[yi], yb.at[yi], y_s.at[d - 1], y_r.at[d - 1], y_dev(d))
+        send(yb.at[yi], yb.at[yi], y_r.at[0], y_dev(d))
     arrived(rres.at[1 - yh], r_r.at[0])
     arrived(gains.at[1 - yh], r_r.at[1])
     base = [dot(pm[...], rres[b]) for b in range(2)]
-    for d in NEAR:
-        arrived(yb.at[(yi - d + 4) % 4], y_r.at[d - 1])
+    arrived(yb.at[pl.ds(0, 3)], y_r.at[0])
     squares = jnp.zeros((64, 1), f32)
     for b in range(2):
         h = base[b] + (yb[2 * b].astype(f32) + yb[2 * b + 1].astype(f32))
@@ -371,7 +354,7 @@
     ss[0, :, 0:64] = jnp.sum(jnp.where(ii == jj, squares, 0.0), axis=0, keepdims=True)
     ss[0, :, 64:128] = jnp.zeros((1, 64), f32)
     for d in ORDER:
-        send(ss.at[0], ss.at[d], n_s.at[d - 1], n_r.at[d - 1], q_dev(d))
+        send(ss.at[0], ss.at[d], n_r.at[0], q_dev(d))
 
     for n in range(2, 6):
         rest[n].wait()
@@ -397,20 +380,18 @@
             sums[n] = values[n] if sums[n] is None else sums[n] + values[n]
 
     def squares_q():
-        for d in NEAR:
-            arrived(ss.at[d], n_r.at[d - 1])
+        arrived(ss.at[pl.ds(1, 3)], n_r.at[0])
         ss[4] = ss[0] + ss[1] + ss[2] + ss[3]
         for d in ORDER:
-            send(ss.at[4], ss.at[4 + d], n_s.at[2 + d], n_r.at[2 + d], p_dev(d))
+            send(ss.at[4], ss.at[4 + d], n_r.at[1], p_dev(d))
 
     def squares_p():
-        for d in NEAR:
-            arrived(ss.at[4 + d], n_r.at[2 + d])
+        arrived(ss.at[pl.ds(5, 3)], n_r.at[1])
         ss[8] = ss[4] + ss[5] + ss[6] + ss[7]
-        send(ss.at[8], ss.at[9], n_s.at[6], n_r.at[6], core)
-
-    gather(gb, dq_s, dq_r, dp_s, dp_r, dc_s, dc_r, up_batch, squares_q, squares_p)
-    arrived(ss.at[9], n_r.at[6])
+        send(ss.at[8], ss.at[9], n_r.at[2], core)
+
+    gather(gb, True, dq_r, dp_r, dc_r, up_batch, squares_q, squares_p)
+    arrived(ss.at[9], n_r.at[2])
     whole = (ss[8] + ss[9])[:, 0:64]
     total = jnp.sum(jnp.where(ii == jj, whole, 0.0), axis=1, keepdims=True)
     scale = lax.rsqrt(total * (1.0 / D) + EPS)
@@ -449,19 +430,19 @@
     def down_other(d):
         for n in range(4):
             ecs[d, n] = down(oc, (q + d) % 4, sq, n, sp).astype(bf16)
-        send(ecs.at[d], ecr.at[d], e0_s.at[d], e0_r.at[d], core)
+        send(ecs.at[d], ecr.at[d], e0_r.at[d], core)
 
     def down_own(d):
-        mine = [down(c, (p + d) % 4, sp, n, sq) for n in range(4)]
+        places = [(q + dq) % 4 for dq in ORDER + (0,)]
+        mine = [down(c, (p + d) % 4, sp, n, sq) for n in places]
         arrived(ecr.at[d], e0_r.at[d])
-        for n in range(4):
-            value = mine[n] + ecr[d, n].astype(f32)
-            if d:
-                e1s[d - 1, n] = value.astype(bf16)
+        for dq, n, value in zip(ORDER + (0,), places, mine):
+            value = value + ecr[d, n].astype(f32)
+            if d or dq:
+                e1s[d, dq] = value.astype(bf16)
+                send(e1s.at[d, dq], e1r.at[4 * d + dq], e1_r.at[0], pq_dev(d, dq))
             else:
-                e1o[n] = value
-        if d:
-            send(e1s.at[d - 1], e1r.at[d - 1], e1_s.at[d - 1], e1_r.at[d - 1], p_dev(d))
+                e1o[...] = value
 
     down_other(2)
     down_other(1)
@@ -471,36 +452,23 @@
     down_own(1)
     down_own(3)
     down_own(0)
-    for d in NEAR:
-        arrived(e1r.at[d - 1], e1_r.at[d - 1])
-    kept = None
-    for d in ORDER + (0,):
-        n = (q + d) % 4
-        value = e1o[n]
-        for s in range(3):
-            value = value + e1r[s, n].astype(f32)
-        if d:
-            e2s[d - 1] = value.astype(bf16)
-            send(e2s.at[d - 1], e2r.at[d - 1], e2_s.at[d - 1], e2_r.at[d - 1], q_dev(d))
-        else:
-            kept = value
-    for d in NEAR:
-        arrived(e2r.at[d - 1], e2_r.at[d - 1])
-        kept = kept + e2r[d - 1].astype(f32)
+    arrived(e1r.at[pl.ds(1, 15)], e1_r.at[0])
+    kept = e1o[...]
+    for n in range(1, 16):
+        kept = kept + e1r[n].astype(f32)
     for b in range(2):
         e3s[b] = kept[:, b * 128 : (b + 1) * 128].astype(bf16)
     for d in ORDER:
         to_block = ((yi + d) % 4) // 2
-        send(e3s.at[to_block], e3r.at[yi], e3_s.at[d - 1], e3_r.at[d - 1], y_dev(d))
+        send(e3s.at[to_block], e3r.at[yi], e3_r.at[0], y_dev(d))
     e3r[yi] = e3s[yh]
-    for d in NEAR:
-        arrived(e3r.at[(yi - d + 4) % 4], e3_r.at[d - 1])
+    arrived(e3r.at[pl.ds(0, 3)], e3_r.at[0])
     lowered = (e3r[0].astype(f32) + e3r[1].astype(f32)) + (e3r[2].astype(f32) + e3r[3].astype(f32))
     result = (hid[yh] + lowered).astype(bf16)
     out_ref[...] = dot(pt[...], result).astype(bf16)
 
-    for src, sem in sent:
-        pltpu.make_async_copy(src, src, sem).wait()
+    arrived(ss.at[pl.ds(0, tiny[0] // 512)], sem_s.at[1])
+    arrived(sg.at[:, pl.ds(0, big[0] // 512)], sem_s.at[0])
 
 
 def shards(
@@ -509,10 +477,10 @@
     gate_signs, up_signs, down_signs, delta_scale,
 ):
     hbm = pl.BlockSpec(memory_space=pltpu.HBM)
-    smem = pl.BlockSpec(memory_space=pltpu.SMEM)
     vm = pltpu.VMEM
     dma = pltpu.SemaphoreType.DMA
     scratch = [
+        pltpu.SMEM((2,), i32), pltpu.SMEM((2, 4), f32),
         vm((1, 64), i32), vm((64, 64), i32), vm((64, 4096), bf16), vm((64, 4096), bf16),
         vm((2, SLOTS, 512), bf16), vm((2, SLOTS, 512), bf16), vm((64, 512), bf16),
         vm((64, 512), bf16), vm((64, 64), f32), vm((64, 64), bf16), vm((64, 64), bf16),
@@ -522,26 +490,21 @@
         vm((2, 64, 128), bf16), vm((2, 1, 128), f32),
         vm((4, 9, 32, 128), bf16), vm((4, 9, 32, 128), bf16),
         vm((4, 9, 32, 128), bf16), vm((3, 9, 32, 128), bf16),
-        vm((4, 3, 32, 128), bf16), vm((2, 4, 3, 32, 128), bf16),
+        vm((4, 3, 32, 128), bf16), vm((8, 3, 32, 128), bf16),
         vm((2, 4, 4, 32, 256), bf16), vm((4, 64, 128), bf16), vm((2, 64, 128), f32),
         vm((2, 4, 4, 64, 256), bf16), vm((10, 1, 128), f32),
-        vm((4, 4, 64, 256), bf16), vm((4, 4, 64, 256), bf16), vm((4, 64, 256), f32),
-        vm((3, 4, 64, 256), bf16), vm((3, 4, 64, 256), bf16),
-        vm((3, 64, 256), bf16), vm((3, 64, 256), bf16),
+        vm((4, 4, 64, 256), bf16), vm((4, 4, 64, 256), bf16), vm((64, 256), f32),
+        vm((4, 4, 64, 256), bf16), vm((16, 64, 256), bf16),
         vm((2, 64, 128), bf16), vm((4, 64, 128), bf16),
-        dma((19,)), dma((4,)), dma((4,)), dma((3,)), dma((3,)), dma((2, 4)), dma((2, 4)),
-        dma((2,)), dma((2,)),
-        dma((3,)), dma((3,)), dma((3, 4)), dma((3, 4)), dma((4, 4)), dma((4, 4)),
-        dma((3,)), dma((3,)),
-        dma((3,)), dma((3,)), dma((3, 4)), dma((3, 4)), dma((4, 4)), dma((4, 4)),
-        dma((7,)), dma((7,)),
-        dma((4,)), dma((4,)), dma((3,)), dma((3,)), dma((3,)), dma((3,)), dma((3,)), dma((3,)),
+        dma((19,)), dma((2,)), dma((4,)), dma((1,)), dma((1,)), dma((2,)),
+        dma((3,)), dma((4,)), dma((4,)), dma((1,)), dma((3,)), dma((4,)), dma((4,)), dma((3,)),
+        dma((4,)), dma((1,)), dma((1,)),
     ]
     return pl.pallas_call(
         layer,
         name="layer",
         out_shape=pltpu.VMEM((64, 128), bf16),
-        in_specs=[hbm, hbm, smem, smem] + [hbm] * 15,
+        in_specs=[hbm] * 19,
         out_specs=pl.BlockSpec(memory_space=pltpu.VMEM),
         scratch_shapes=scratch,
         compiler_params=pltpu.CompilerParams(

time: 63.6 us -> 57.9 us (0.910)
  Pallas kernels: 62.9 us -> 56.7 us
    pallas_call x1, Pallas kernels: 62.9 us -> 56.7 us  [shards(): pl.pallas_call(layer, name='layer', out_shape=pltpu.VMEM((64, 128), bf16)...]
where the time goes in v3:
time: 57.9 us; the launch traced here: 57.3 us
  Pallas kernels  56.7 us (98%)
  local copies, waits for them, and re-layouts  0.61 us (1%)
    pallas_call x1, Pallas kernels, shards(): pl.pallas_call(layer, name='layer', out_shape=pltpu.VMEM((64, 128), bf16)...  56.7 us

profile of v3, /device:TPU:0, one launch (start us, length us, event | category | flops | bytes accessed | tf_op | source)
XLA Modules:
  0.0 57.3 jit_solution(4076272735136027711)
XLA Ops:
  0.0 56.7 %layer.1 = bf16[64,128]{1,0:T(8,128)(2,1)S(1)} custom-call(s32[1,64]{1,0:T(1,128)} %bitcast.2, s32[64,64]{1,0:T(8,128)} %mask_h.1, s32[2]{0:T(128)} %lens_h.1, f32[2,4]{1,0:T(2,128)} %dsc_h.1, bf16[64,128]{1,0:T(8,128)(2,1)} %res_h.1, bf16[64,4096]{1,0:T(8,128)(2,1)} %q_h.1, bf16[64,512]{1,0:T(8,128)(2,1)} %dk_h.1, bf16[64,512]{1,0:T(8,128)(2,1)} %dv_h.1, ...), custom_call_target="tpu_custom_call" | custom-call | tf_op jit(solution)/shard_map/layer/pallas_call | solution.py:503
  56.7 0.6 %copy.21 = bf16[64,128]{1,0:T(8,128)(2,1)} copy(bf16[64,128]{1,0:T(8,128)(2,1)S(1)} %layer.1) | data formatting | bytes 32768

commit v4 on v3

v4 whole, which is shorter than its diff:
```python
import functools

import jax
import jax.numpy as jnp
from jax import lax
from jax.experimental import pallas as pl
from jax.experimental.pallas import tpu as pltpu
from jax.sharding import PartitionSpec as P

D = 8192
FF = 16384
HEAD = 128
SLOTS = 512
NEG = -1e30
LOG2E = 1.4426950408889634
EPS = 1e-05
MESH = pl.DeviceIdType.MESH
f32, bf16, i32 = jnp.float32, jnp.bfloat16, jnp.int32
ORDER = (2, 1, 3)
NEAR = (1, 3, 2)


def dot(a, b, dims=((1,), (0,))):
    return lax.dot_general(a, b, (dims, ((), ())), preferred_element_type=f32)


def mult(v, n):
    return pl.multiple_of(v, n)


def lanes():
    return lax.broadcasted_iota(i32, (32, 128), 1)


def split(st):
    hi = st.astype(bf16).astype(f32)
    mid = (st - hi).astype(bf16).astype(f32)
    lo = st - hi - mid
    lane = lanes()
    return jnp.where(
        lane < 32, hi, jnp.where(lane < 64, mid, jnp.where(lane < 96, lo, 0.0))
    ).astype(bf16)


def join(block):
    v = block.astype(f32)
    v = v + pltpu.roll(v, 32, 1)
    return v + pltpu.roll(v, 64, 1)


def blend(stats):
    top = functools.reduce(jnp.maximum, stats)
    parts = [jnp.exp(s - top) for s in stats]
    total = functools.reduce(jnp.add, parts)
    inverse = 1.0 / total
    return [w * inverse for w in parts], top + jnp.log(total)


def mixed_of(factors, blocks, k):
    terms = [f[:, k : k + 1] * b for f, b in zip(factors, blocks)]
    return functools.reduce(jnp.add, terms)


def layer(
    ids_h, mask_h, lens_h, dsc_h, res_h, q_h, dk_h, dv_h, ck_h, cv_h, wo_h, so_h, gain_h,
    wg_h, wu_h, wd_h, sg_h, su_h, sd_h,
    out_ref,
    lens, dsc, ids, mask, qraw, qs, kc, vc, dk, dv, vis, pm, pt, wo, so, wg, wu, wd, sg, su, sd, ro, rg, ru, rd,
    rres, gains, acs, acr, a1s, a1r, a2s, a2r, ab, yb, hid, his, gb, ss,
    e1o, e1s, e1r, e3s, e3r,
    ls, sem_s, w_s, c_r, a1_r, a2_r, r_r, w_r, b_r, y_r, d_r, n_r, h_r, e1_r, e3_r,
):
    kv, ctx = lax.axis_index("kv"), lax.axis_index("ctx")
    c = ctx % 2
    yh = (ctx // 2) % 2
    x = (ctx // 4) % 4
    z = ctx // 16
    p = z + c * (x - z)
    q = x + c * (z - x)
    sp, sq = 16 - 12 * c, 4 + 12 * c
    yi = yh * 2 + kv
    oc = 1 - c

    core = (kv, ctx + 1 - 2 * c)

    def across(dev):
        return (dev[0], dev[1] + 1 - 2 * c)

    def p_dev(d):
        return (kv, ctx + ((p + d) % 4 - p) * sp)

    def q_dev(d):
        return (kv, ctx + ((q + d) % 4 - q) * sq)

    def y_dev(d):
        to = (yi + d) % 4
        return (to % 2, ctx + (to // 2 - yh) * 2)

    def pq_dev(d, e):
        return (kv, p_dev(d)[1] + q_dev(e)[1] - ctx)

    def qy_dev(d, e):
        return (kv, q_dev(d)[1] + e * (2 - 4 * yh))

    near_step = 3 - 2 * (yi % 2)
    near = y_dev(near_step)

    barrier = pltpu.get_barrier_semaphore()
    peers = [core] + [p_dev(d) for d in NEAR] + [q_dev(d) for d in NEAR] + [y_dev(d) for d in NEAR]
    peers += [qy_dev(d, 1) for d in NEAR]
    peers += [pq_dev(d, e) for d in NEAR for e in NEAR]
    peers += [across(y_dev(d)) for d in NEAR]
    def load(n, src, dst):
        copy = pltpu.make_async_copy(src, dst, ls.at[n])
        copy.start()
        return copy

    first = [load(0, ids_h, ids), load(1, q_h, qraw), load(17, lens_h, lens), load(18, dsc_h, dsc)]
    for peer in peers:
        pl.semaphore_signal(barrier, inc=1, device_id=peer, device_id_type=MESH)
    load(2, ck_h.at[oc], kc.at[oc])
    load(2, cv_h.at[oc], vc.at[oc])
    load(3, ck_h.at[c], kc.at[c])
    load(3, cv_h.at[c], vc.at[c])
    small = [
        load(4, mask_h, mask), load(5, dk_h, dk), load(6, dv_h, dv),
        load(7, res_h, rres.at[yh, c]), load(8, gain_h, gains.at[yh, c]),
    ]

    big, tiny = [0], [0]

    def send(src, dst, r_sem, to, s_sem=None):
        if s_sem is None:
            size = 1
            for n in src.shape:
                size *= n
            small_one = src.dtype == f32
            (tiny if small_one else big)[0] += size * (4 if small_one else 2)
            s_sem = sem_s.at[1 if small_one else 0]
        pltpu.make_async_remote_copy(
            src_ref=src, dst_ref=dst, send_sem=s_sem, recv_sem=r_sem,
            device_id=to, device_id_type=MESH,
        ).start()

    def arrived(dst, sem):
        pltpu.make_async_copy(dst, dst, sem).wait()

    for copy in first:
        copy.wait()
    row = jnp.broadcast_to(ids[...].astype(f32), (64, 64))
    ii = lax.broadcasted_iota(i32, (64, 64), 0)
    jj = lax.broadcasted_iota(i32, (64, 64), 1)
    col = jnp.sum(jnp.where(ii == jj, row, 0.0), axis=1, keepdims=True)
    same = jnp.where(row == col, 1.0, 0.0)
    pos_col = jnp.sum(jnp.where(jj < ii, same, 0.0), axis=1, keepdims=True) + 32.0 * col
    pos_row = jnp.sum(jnp.where(ii < jj, same, 0.0), axis=0, keepdims=True) + 32.0 * row[:1]
    pt[...] = jnp.where(pos_col == jj.astype(f32), 1.0, 0.0).astype(bf16)
    pm[...] = jnp.where(pos_row == ii.astype(f32), 1.0, 0.0).astype(bf16)

    for n in range(4):
        at = pl.ds(n * 1024, 1024)
        qs[:, at] = dot(pm[...], qraw[:, at]).astype(bf16)

    factor = HEAD ** (-0.5)
    c32, o32 = mult(c * 32, 32), mult(oc * 32, 32)
    first_slot = ctx * SLOTS

    def attend(t, t32, g):
        rows = jnp.concatenate(
            [qs[pl.ds(t32, 32), pl.ds(mult((g * 8 + k) * 128, 128), 128)] for k in range(8)], axis=0
        )
        at = pl.ds(mult(g * 128, 128), 128)
        s = dot(rows, kc[t, :, at], ((1,), (1,)))
        live = lax.broadcasted_iota(i32, (1, SLOTS), 1) + first_slot < lens[t]
        s = jnp.where(live, s, NEG)
        m = jnp.max(s, axis=1, keepdims=True)
        m = jnp.where(m > 0.5 * NEG, m, 0.0)
        e = jnp.exp2((s - m) * (factor * LOG2E))
        l = jnp.sum(e, axis=1, keepdims=True)
        o = dot(e.astype(bf16), vc[t, :, at])
        some = l > 0.0
        safe = jnp.where(some, l, 1.0)
        o = o * (1.0 / safe)
        lse = jnp.where(some, m * factor + jnp.log(safe), NEG)
        lane = lanes() % 32
        st = jnp.zeros((32, 128), f32)
        for k in range(8):
            st = jnp.where(lane == k, lse[k * 32 : (k + 1) * 32], st)
        return o, st

    arrived(kc, ls.at[2])
    group = [
        (wo_h, wo, so_h, so, ro, 0, D), (wg_h, wg, sg_h, sg, rg, 1, D),
        (wu_h, wu, su_h, su, ru, 2, D), (wd_h, wd, sd_h, sd, rd, 3, FF),
    ]
    rest = [
        (load(9 + 2 * n, one[0], one[1]), load(10 + 2 * n, one[2], one[3]))
        for n, one in enumerate(group)
    ]

    def combine(n):
        _, base_w, _, both, remote, at_scale, width = group[n]
        for copy in rest[n]:
            copy.wait()
        scales = [dsc[t, at_scale] * width ** (-0.5) for t in range(2)]
        count, piece = (base_w.shape[0], 256) if n < 3 else (base_w.shape[1], 256)

        @pl.loop(0, count // piece)
        def _(i):
            part = pl.ds(mult(i * piece, piece), piece)
            at = (part, slice(None)) if n < 3 else (slice(None), part)
            base_part = base_w[at].astype(f32)
            for t in range(2):
                total_part = base_part + scales[t] * both[(t, *at)].astype(f32)
                both[(t, *at)] = total_part.astype(bf16)

        send(both.at[oc], remote, w_r.at[n], core, w_s.at[n])

    def other_block(d):
        o, st = attend(oc, o32, (q + d) % 4)
        for k in range(8):
            acs[d, k] = o[k * 32 : (k + 1) * 32].astype(bf16)
        acs[d, 8] = split(st)

    def other_send(d):
        send(acs.at[d], acr.at[d], c_r.at[d], core)

    for d in ORDER + (0,):
        other_block(d)
    pl.semaphore_wait(barrier, len(peers))
    for d in ORDER + (0,):
        other_send(d)
    arrived(kc, ls.at[3])
    for copy in small:
        copy.wait()
    for n, to in enumerate((near, core, across(near))):
        send(rres.at[yh, c], rres.at[yh, c], r_r.at[0], to)
        send(gains.at[yh, c], gains.at[yh, c], r_r.at[1], to)

    def merge(d, o, st):
        factors, lse = blend([st, join(acr[d, 8])])
        for k in range(8):
            blocks = [o[k * 32 : (k + 1) * 32], acr[d, k].astype(f32)]
            a1s[d, k] = mixed_of(factors, blocks, k).astype(bf16)
        a1s[d, 8] = split(lse)
        if d:
            send(a1s.at[d], a1r.at[d - 1], a1_r.at[0], p_dev(d))

    pending = []
    for d in ORDER + (0,):
        pending.append((d, *attend(c, c32, (p + d) % 4)))
        if len(pending) > 1:
            arrived(acr.at[pending[0][0]], c_r.at[pending[0][0]])
            merge(*pending.pop(0))
    arrived(acr.at[0], c_r.at[0])
    merge(*pending.pop(0))

    vis[...] = dot(pm[...], mask[...].astype(f32).astype(bf16))
    head0 = p * 8 + q * 2
    rows = jnp.concatenate(
        [qs[pl.ds(c32, 32), pl.ds(mult((head0 + k) * 128, 128), 128)] for k in range(2)], axis=0
    )
    at_p = pl.ds(mult(p * 128, 128), 128)
    seen = jnp.concatenate([vis[pl.ds(c32, 32), :]] * 2, axis=0) > 0.5
    s = jnp.where(seen, dot(rows, dk[:, at_p], ((1,), (1,))) * factor, NEG)
    m = jnp.max(s, axis=1, keepdims=True)
    e = jnp.where(seen, jnp.exp(s - m), 0.0)
    l = jnp.sum(e, axis=1, keepdims=True)
    draft_o = dot(e.astype(bf16), dv[:, at_p]) * (1.0 / l)
    lse = m + jnp.log(l)
    draft_st = jnp.where(lanes() % 32 == 0, lse[:32], lse[32:])

    combine(0)

    arrived(a1r, a1_r.at[0])
    sources = [a1s.at[0]] + [a1r.at[n] for n in range(3)]
    factors, lse = blend([join(s[8]) for s in sources])
    keep = None
    for d in ORDER + (0,):
        to_q = (q + d) % 4
        shift = (128 - 2 * to_q) % 128
        turned = [pltpu.roll(f, shift, 1) for f in factors]
        heads = [
            mixed_of(turned, [s[2 * to_q + k].astype(f32) for s in sources], k) for k in range(2)
        ]
        st = pltpu.roll(lse, shift, 1)
        a2s[d, 0] = heads[0].astype(bf16)
        a2s[d, 1] = heads[1].astype(bf16)
        a2s[d, 2] = split(st)
        for e in (1, 0):
            if d or e:
                send(a2s.at[d], a2r.at[4 * e + d], a2_r.at[0], qy_dev(d, e))
        if not d:
            keep = (heads, st)

    others = [(0, 1), (0, 3), (1, 0), (1, 1), (1, 3), (0, 2), (1, 2)]
    combine(1)
    combine(2)
    arrived(a2r.at[pl.ds(1, 7)], a2_r.at[0])
    factors, _ = blend([keep[1]] + [join(a2r[4 * e + d, 2]) for e, d in others] + [draft_st])
    for k in range(2):
        blocks = [keep[0][k]] + [a2r[4 * e + d, k].astype(f32) for e, d in others]
        blocks.append(draft_o[k * 32 : (k + 1) * 32])
        ab[p, q, :, k * 128 : (k + 1) * 128] = mixed_of(factors, blocks, k).astype(bf16)

    def spread(buf, r_sem):
        mine = buf.at[p, q]
        for dp in (0,) + ORDER:
            for dq in ORDER + (0,):
                if dp or dq:
                    send(mine, mine, r_sem.at[dp], pq_dev(dp, dq))

    def row_in(buf, dp, r_sem):
        at_p = (p - dp + 4) % 4
        if dp:
            arrived(buf.at[at_p], r_sem.at[dp])
        else:
            arrived(buf.at[at_p, pl.ds(0, 3)], r_sem.at[0])
        return at_p

    spread(ab, b_r)
    combine(3)
    arrived(ro, w_r.at[0])
    projected = None
    for dp in (0,) + NEAR:
        at_p = row_in(ab, dp, b_r)
        lhs = jnp.concatenate([ab[at_p, n] for n in range(4)], axis=1)
        at = pl.ds(mult(at_p * 1024, 1024), 1024)
        value = dot(lhs, jnp.concatenate([so[c, at, :], ro[at, :]], axis=1))
        projected = value if projected is None else projected + value
    for n, t in ((0, c), (1, oc)):
        value = projected[:, n * 128 : (n + 1) * 128]
        yb[yi, :, pl.ds(mult(t * 128, 128), 128)] = value.astype(bf16)

    for d in ORDER:
        send(yb.at[yi], yb.at[yi], y_r.at[0], y_dev(d))
    arrived(qs.at[:, pl.ds(0, 384)], r_r.at[0])
    arrived(ss.at[pl.ds(0, 3)], r_r.at[1])
    own_rows = pm[pl.ds(c32, 32), :]
    base = [[dot(own_rows, rres[b, t]) for t in range(2)] for b in range(2)]
    arrived(yb.at[pl.ds(0, 3)], y_r.at[0])
    squares = jnp.zeros((32, 1), f32)
    for b in range(2):
        for t in range(2):
            at = slice(t * 128, (t + 1) * 128)
            h = base[b][t] + (yb[2 * b, :, at].astype(f32) + yb[2 * b + 1, :, at].astype(f32))
            his[b, t] = h
            gb[p, q, :, (2 * b + t) * 128 : (2 * b + t + 1) * 128] = (h * gains[b, t]).astype(bf16)
            squares = squares + jnp.sum(h * h, axis=1, keepdims=True)
    eye = lax.broadcasted_iota(i32, (32, 128), 0) == lanes()
    place = p * 4 + q
    ss[place] = jnp.sum(jnp.where(eye, squares, 0.0), axis=0, keepdims=True)
    for dp in ORDER + (0,):
        for dq in ORDER + (0,):
            if dp or dq:
                send(ss.at[place], ss.at[place], n_r.at[0], pq_dev(dp, dq))
    spread(gb, d_r)
    hid[c] = his[yh, c]
    send(his.at[yh, oc], hid.at[c], h_r.at[0], core, w_s.at[4])

    arrived(rg, w_r.at[1])
    arrived(ru, w_r.at[2])
    sums = [None] * 2
    for dp in (0,) + NEAR:
        at_p = row_in(gb, dp, d_r)
        if dp == 2:
            arrived(ss.at[pl.ds(0, 15)], n_r.at[0])
            whole = functools.reduce(jnp.add, [ss[n] for n in range(16)])
            total = jnp.sum(jnp.where(eye, whole, 0.0), axis=1, keepdims=True)
            scale = lax.rsqrt(total * (1.0 / D) + EPS)
        lhs = jnp.concatenate([gb[at_p, n] for n in range(4)], axis=1)

        def rows(*ref):
            parts = []
            for n in range(4):
                at = pl.ds(mult((at_p * sp + n * sq) * 128, 512), 512)
                parts.append(ref[0][(*ref[1:], at, slice(None))])
            return jnp.concatenate(parts, axis=0)

        for n, (left, right) in enumerate((((sg, c), (su, c)), ((rg,), (ru,)))):
            value = dot(lhs, jnp.concatenate([rows(*left), rows(*right)], axis=1))
            sums[n] = value if sums[n] is None else sums[n] + value

    parts = []
    for n in range(2):
        gate, up = sums[n][:, :128] * scale, sums[n][:, 128:] * scale
        parts.append((gate / (1.0 + jnp.exp(-gate)) * up).astype(bf16))
    active = jnp.concatenate(parts, axis=1)

    arrived(rd, w_r.at[3])
    for dp in ORDER + (0,):
        for dq in ORDER + (0,):
            at = pl.ds(mult(((p + dp) % 4 * sp + (q + dq) % 4 * sq) * 128, 512), 512)
            value = dot(active, jnp.concatenate([sd[c, :, at], rd[:, at]], axis=0))
            if dp or dq:
                e1s[dp, dq] = value.astype(bf16)
                send(e1s.at[dp, dq], e1r.at[4 * dp + dq], e1_r.at[0], pq_dev(dp, dq))
            else:
                e1o[...] = value
    arrived(e1r.at[pl.ds(1, 15)], e1_r.at[0])
    kept = e1o[...]
    for n in range(1, 16):
        kept = kept + e1r[n].astype(f32)
    for b in range(2):
        for t in range(2):
            at = (2 * b + t) * 128
            e3s[b, t] = kept[:, at : at + 128].astype(bf16)
    for d in ORDER + (0,):
        to_block = ((yi + d) % 4) // 2
        send(e3s.at[to_block, oc], e3r.at[c, yi], e3_r.at[0], across(y_dev(d)))
        if d:
            send(e3s.at[to_block, c], e3r.at[c, yi], e3_r.at[0], y_dev(d))
    e3r[c, yi] = e3s[yh, c]
    arrived(hid.at[oc], h_r.at[0])
    arrived(a1s.at[0, pl.ds(0, 7)], e3_r.at[0])
    results = []
    for t in range(2):
        got = [e3r[t, n].astype(f32) for n in range(4)]
        results.append((hid[t] + ((got[0] + got[1]) + (got[2] + got[3]))).astype(bf16))
    out_ref[...] = dot(pt[...], jnp.concatenate(results, axis=0)).astype(bf16)

    arrived(ss.at[pl.ds(0, tiny[0] // 512)], sem_s.at[1])
    arrived(sg.at[:, pl.ds(0, big[0] // 512)], sem_s.at[0])
    for n, one in enumerate(group):
        arrived(one[4], w_s.at[n])
    arrived(hid.at[0], w_s.at[4])


def shards(
    residual, queries, draft_keys, draft_values, cache_keys, cache_values, tenant_ids, tree_mask,
    cache_lengths, out_weight, out_signs, norm_gain, gate_weight, up_weight, down_weight,
    gate_signs, up_signs, down_signs, delta_scale,
):
    hbm = pl.BlockSpec(memory_space=pltpu.HBM)
    vm = pltpu.VMEM
    dma = pltpu.SemaphoreType.DMA
    scratch = [
        pltpu.SMEM((2,), i32), pltpu.SMEM((2, 4), f32),
        vm((1, 64), i32), vm((64, 64), i32), vm((64, 4096), bf16), vm((64, 4096), bf16),
        vm((2, SLOTS, 512), bf16), vm((2, SLOTS, 512), bf16), vm((64, 512), bf16),
        vm((64, 512), bf16), vm((64, 64), f32), vm((64, 64), bf16), vm((64, 64), bf16),
        vm((4096, 128), bf16), vm((2, 4096, 128), bf16), vm((8192, 128), bf16),
        vm((8192, 128), bf16), vm((128, 8192), bf16), vm((2, 8192, 128), bf16),
        vm((2, 8192, 128), bf16), vm((2, 128, 8192), bf16),
        vm((4096, 128), bf16), vm((8192, 128), bf16), vm((8192, 128), bf16), vm((128, 8192), bf16),
        vm((2, 2, 64, 128), bf16), vm((2, 2, 1, 128), f32),
        vm((4, 9, 32, 128), bf16), vm((4, 9, 32, 128), bf16),
        vm((4, 9, 32, 128), bf16), vm((3, 9, 32, 128), bf16),
        vm((4, 3, 32, 128), bf16), vm((8, 3, 32, 128), bf16),
        vm((4, 4, 32, 256), bf16), vm((4, 32, 256), bf16), vm((2, 32, 128), f32),
        vm((2, 2, 32, 128), f32), vm((4, 4, 32, 512), bf16), vm((20, 1, 128), f32),
        vm((32, 512), f32), vm((4, 4, 32, 512), bf16), vm((16, 32, 512), bf16),
        vm((2, 2, 32, 128), bf16), vm((2, 4, 32, 128), bf16),
        dma((19,)), dma((2,)), dma((5,)), dma((4,)), dma((1,)), dma((1,)), dma((2,)), dma((4,)),
        dma((4,)), dma((1,)), dma((4,)), dma((2,)), dma((1,)), dma((1,)), dma((1,)),
    ]
    return pl.pallas_call(
        layer,
        name="layer",
        out_shape=pltpu.VMEM((64, 128), bf16),
        in_specs=[hbm] * 19,
        out_specs=pl.BlockSpec(memory_space=pltpu.VMEM),
        scratch_shapes=scratch,
        compiler_params=pltpu.CompilerParams(
            collective_id=0, has_side_effects=True, vmem_limit_bytes=60 * 1024 * 1024
        ),
    )(
        tenant_ids.reshape(1, 64), tree_mask, cache_lengths, delta_scale, residual, queries,
        draft_keys, draft_values, cache_keys, cache_values, out_weight, out_signs,
        norm_gain.reshape(1, 128), gate_weight, up_weight, down_weight, gate_signs, up_signs,
        down_signs,
    )


def solution(mesh):
    return jax.shard_map(
        shards,
        mesh=mesh,
        in_specs=(
            P(None, "ctx"),
            P(None, "kv"),
            P(None, "kv"),
            P(None, "kv"),
            P(None, "ctx", "kv"),
            P(None, "ctx", "kv"),
            P(),
            P(),
            P(),
            P("kv", "ctx"),
            P(None, "kv", "ctx"),
            P("ctx"),
            P(None, ("kv", "ctx")),
            P(None, ("kv", "ctx")),
            P(("kv", "ctx"), None),
            P(None, None, ("kv", "ctx")),
            P(None, None, ("kv", "ctx")),
            P(None, ("kv", "ctx"), None),
            P(),
        ),
        out_specs=P(None, "ctx"),
        check_vma=False,
    )
```

time: 57.9 us -> 50.4 us (0.87)
  Pallas kernels: 56.7 us -> 48.9 us
    pallas_call x1, Pallas kernels: 56.7 us -> 48.9 us  [shards(): pl.pallas_call(layer, name='layer', out_shape=pltpu.VMEM((64, 128), bf16)...]
where the time goes in v4:
time: 50.4 us; the launch traced here: 49.6 us
  Pallas kernels  48.9 us (97%)
  local copies, waits for them, and re-layouts  0.61 us (1%)
    pallas_call x1, Pallas kernels, shards(): pl.pallas_call(layer, name='layer', out_shape=pltpu.VMEM((64, 128), bf16)...  48.9 us

profile of v4, /device:TPU:0, one launch (start us, length us, event | category | flops | bytes accessed | tf_op | source)
XLA Modules:
  0.0 49.6 jit_solution(7297169911319067871)
XLA Ops:
  0.0 48.9 %layer.1 = bf16[64,128]{1,0:T(8,128)(2,1)S(1)} custom-call(s32[1,64]{1,0:T(1,128)} %bitcast.2, s32[64,64]{1,0:T(8,128)} %mask_h.1, s32[2]{0:T(128)} %lens_h.1, f32[2,4]{1,0:T(2,128)} %dsc_h.1, bf16[64,128]{1,0:T(8,128)(2,1)} %res_h.1, bf16[64,4096]{1,0:T(8,128)(2,1)} %q_h.1, bf16[64,512]{1,0:T(8,128)(2,1)} %dk_h.1, bf16[64,512]{1,0:T(8,128)(2,1)} %dv_h.1, ...), custom_call_target="tpu_custom_call" | custom-call | tf_op jit(solution)/shard_map/layer/pallas_call | solution.py:457
  49.0 0.6 %copy.21 = bf16[64,128]{1,0:T(8,128)(2,1)} copy(bf16[64,128]{1,0:T(8,128)(2,1)S(1)} %layer.1) | data formatting | bytes 32768

commit v5 on v4

--- a/solution.py
+++ b/solution.py
@@ -305,10 +305,12 @@
 
     def spread(buf, r_sem):
         mine = buf.at[p, q]
-        for dp in (0,) + ORDER:
-            for dq in ORDER + (0,):
-                if dp or dq:
-                    send(mine, mine, r_sem.at[dp], pq_dev(dp, dq))
+        far_first = sorted(
+            ((a, b) for a in range(4) for b in range(4) if a or b),
+            key=lambda v: (-min(v[0], 4 - v[0]) - min(v[1], 4 - v[1]), v),
+        )
+        for dp, dq in far_first:
+            send(mine, mine, r_sem.at[dp], pq_dev(dp, dq))
 
     def row_in(buf, dp, r_sem):
         at_p = (p - dp + 4) % 4

time: 50.4 us -> 49.8 us (0.988)
  Pallas kernels: 48.9 us -> 48.3 us
    pallas_call x1, Pallas kernels: 48.9 us -> 48.3 us  [shards(): pl.pallas_call(layer, name='layer', out_shape=pltpu.VMEM((64, 128), bf16)...]
where the time goes in v5:
time: 49.8 us; the launch traced here: 48.9 us
  Pallas kernels  48.3 us (97%)
  local copies, waits for them, and re-layouts  0.61 us (1%)
    pallas_call x1, Pallas kernels, shards(): pl.pallas_call(layer, name='layer', out_shape=pltpu.VMEM((64, 128), bf16)...  48.3 us

profile of v5, /device:TPU:0, one launch (start us, length us, event | category | flops | bytes accessed | tf_op | source)
XLA Modules:
  0.0 48.9 jit_solution(18195006520225097205)
XLA Ops:
  0.0 48.3 %layer.1 = bf16[64,128]{1,0:T(8,128)(2,1)S(1)} custom-call(s32[1,64]{1,0:T(1,128)} %bitcast.2, s32[64,64]{1,0:T(8,128)} %mask_h.1, s32[2]{0:T(128)} %lens_h.1, f32[2,4]{1,0:T(2,128)} %dsc_h.1, bf16[64,128]{1,0:T(8,128)(2,1)} %res_h.1, bf16[64,4096]{1,0:T(8,128)(2,1)} %q_h.1, bf16[64,512]{1,0:T(8,128)(2,1)} %dk_h.1, bf16[64,512]{1,0:T(8,128)(2,1)} %dv_h.1, ...), custom_call_target="tpu_custom_call" | custom-call | tf_op jit(solution)/shard_map/layer/pallas_call | solution.py:459
  48.3 0.6 %copy.21 = bf16[64,128]{1,0:T(8,128)(2,1)} copy(bf16[64,128]{1,0:T(8,128)(2,1)S(1)} %layer.1) | data formatting | bytes 32768
